TPU v7x, 32 devices: a whole 2x2x4 slice. The times are simulated.
32 devices in a mesh: blk: 16 (over z, y, core), rel: 2 (over x).
Axes of the slice: x: 2, y: 2, z: 4, core: 2. Of those that a mesh axis runs over, the one named last changes fastest.
Arguments:
- user_table: float32 [16384, 512], P(('blk', 'rel')), may hold values from -1.5 to 1.5
- user_accum: float32 [16384], P(('blk', 'rel')), may hold values from 1 to 100
- item_table: float32 [32768, 512], P(('blk', 'rel')), may hold values from -1.5 to 1.5
- item_accum: float32 [32768], P(('blk', 'rel')), may hold values from 1 to 100
- relation: bfloat16 [512, 512], replicated, may hold values from -0.25 to 0.25
- relation_accum: float32 [512], replicated, may hold values from 0.5 to 8
- targets: bfloat16 [2, 16384, 2048], P(None, 'blk', 'rel'), may hold values from 0 to 1
Outputs:
- user_table_next: float32 [16384, 512], P(('blk', 'rel'))
- user_accum_next: float32 [16384], P(('blk', 'rel'))
- item_table_next: float32 [32768, 512], P(('blk', 'rel'))
- item_accum_next: float32 [32768], P(('blk', 'rel'))
- relation_step: float32 [512, 512], replicated
- relation_accum_next: float32 [512], replicated
All inputs are finite; a program needn't handle non-finite values.
Results may differ from a plain program's by a relative error of at most 0.0037.
The roundings to bfloat16 on the way count: a program that leaves them out, or rounds other values in their place, can miss the bound.
Values may be sent and summed in bfloat16 or wider, within the bound.
No kernel may reach another device: no remote copies, remote signals or barrier semaphores. Data moves between devices by JAX's collectives and lax.ppermute only.
A program may use at most 64 MiB of HBM per device.

v0:
```python
import functools

import jax
import jax.numpy as jnp
from jax import lax
from jax.experimental import pallas as pl
from jax.experimental.pallas import tpu as pltpu
from jax.sharding import PartitionSpec as P


learn_rate = 0.1
epsilon = 1e-06
narrow = jnp.bfloat16
single = jnp.float32
TILE = 256


def exchange(x, flip, rel_flip):
    blocks, rels = lax.axis_size("blk"), lax.axis_size("rel")
    pairs = [
        (b * rels + r, (b ^ flip) * rels + (r ^ rel_flip)) for b in range(blocks) for r in range(rels)
    ]
    return lax.ppermute(x, ("blk", "rel"), pairs)


def swap(x):
    return exchange(x, 0, 1)


def from_behind(x):
    peers = lax.axis_size("blk")
    return lax.ppermute(x, "blk", [(i, (i + 1) % peers) for i in range(peers)])


def wide(x):
    return x.astype(single)


def dot(a, b, da, db):
    return lax.dot_general(a, b, (((da,), (db,)), ((), ())), preferred_element_type=single)


def as_column(line):
    return jnp.transpose(jnp.broadcast_to(line, (8, line.shape[1])))[:, :1]


def as_line(column):
    return jnp.transpose(jnp.broadcast_to(column, (column.shape[0], 128)))[:1, :]


def adagrad_rows(table, accum, grads):
    accum_next = accum + jnp.sum(grads * grads, axis=1, keepdims=True) * (1.0 / grads.shape[1])
    return table - grads * (learn_rate * lax.rsqrt(accum_next + epsilon)), accum_next


def whole(*shape):
    return pl.BlockSpec(shape, lambda *_: (0,) * len(shape))


def shape(dtype, *dims):
    return jax.ShapeDtypeStruct(dims, dtype)


def call(body, grid, in_specs, out_specs, out_shape, scratch, flops, prefetch=0, limit=63):
    return pl.pallas_call(
        body,
        grid_spec=pltpu.PrefetchScalarGridSpec(
            num_scalar_prefetch=prefetch,
            grid=grid,
            in_specs=in_specs,
            out_specs=out_specs,
            scratch_shapes=scratch,
        ),
        out_shape=out_shape,
        compiler_params=pltpu.CompilerParams(
            dimension_semantics=("arbitrary",) * len(grid), vmem_limit_bytes=limit << 20
        ),
        cost_estimate=pl.CostEstimate(flops=flops, bytes_accessed=4 << 20, transcendentals=0),
    )


def errors_of(scores, labels):
    return (jax.nn.sigmoid(scores) - wide(labels)).astype(narrow)


def anywhere():
    return pl.BlockSpec(memory_space=pl.ANY)


def manual(body, in_specs, out_specs, out_shape, scratch, copies, flops):
    return pl.pallas_call(
        body,
        in_specs=in_specs,
        out_specs=out_specs,
        out_shape=out_shape,
        scratch_shapes=[*scratch, pltpu.SemaphoreType.DMA((copies,))],
        compiler_params=pltpu.CompilerParams(vmem_limit_bytes=63 << 20),
        cost_estimate=pl.CostEstimate(flops=flops, bytes_accessed=4 << 20, transcendentals=0),
    )


class Copies:
    def __init__(self, sems):
        self.sems, self.used, self.out = sems, 0, []

    def start(self, source, target):
        copy = pltpu.make_async_copy(source, target, self.sems.at[self.used])
        self.used += 1
        copy.start()
        return copy

    def send(self, source, target):
        self.out.append(self.start(source, target))

    def finish(self):
        for copy in self.out:
            copy.wait()


def tiles(count):
    return [slice(k * TILE, (k + 1) * TILE) for k in range(count // TILE)]


def first_body(place, users, items, relation, labels, items_b, mapped, anchor, errors, grad, grad_b):
    j = pl.program_id(0)

    @pl.when(j == 0)
    def _():
        anchor[...] = dot(users[...], relation[...], 1, 0).astype(narrow)

    block = items[...].astype(narrow)
    items_b[...] = block
    mapped[...] = dot(block, relation[...], 1, 1).astype(narrow)
    found = errors_of(dot(anchor[...], block, 1, 1), labels[...])
    errors[...] = found
    part = dot(found, mapped[...], 1, 0)

    @pl.when(j == 0)
    def _():
        grad[...] = part

    @pl.when(j > 0)
    def _():
        grad[...] += part

    @pl.when(j == pl.num_programs(0) - 1)
    def _():
        grad_b[...] = grad[...].astype(narrow)


def first_own(place, users, items, relation, targets, turn):
    n, d = users.shape
    m = items.shape[0]
    tile = pl.BlockSpec((TILE, d), lambda j, place: (j, 0))
    labels = pl.BlockSpec((None, n, TILE), lambda j, place: (turn, place[0], j))
    return call(
        first_body,
        (m // TILE,),
        [whole(n, d), tile, whole(d, d), labels],
        [
            tile,
            tile,
            whole(n, d),
            pl.BlockSpec((n, TILE), lambda j, place: (0, j)),
            whole(n, d),
            whole(n, d),
        ],
        [
            shape(narrow, m, d),
            shape(narrow, m, d),
            shape(narrow, n, d),
            shape(narrow, n, m),
            shape(single, n, d),
            shape(narrow, n, d),
        ],
        [],
        2 * n * d * d + 2 * m * d * d + 4 * n * m * d,
        prefetch=1,
    )(place, users, items, relation, targets)


def peer_body(
    place, sums, users, relation, items_b, targets, mapped, errors_o, anchor_o, table,
    errors_p, grad_b, items_next, sums_next,
    v_users, v_relation, v_items, v_labels, v_mapped, v_errors_o, v_anchor_o, v_table,
    v_anchor, v_errors, v_grad, v_next, sems,
    turn,
):
    go = Copies(sems)
    n = users.shape[0]
    peer_rows = pl.ds(pl.multiple_of((1 - place[0]) * n, n), n)
    get_users = go.start(users, v_users)
    get_relation = go.start(relation, v_relation)
    get_items = go.start(items_b, v_items)
    get_labels = go.start(targets.at[turn, peer_rows], v_labels)
    get_mapped = go.start(mapped, v_mapped)
    get_errors = go.start(errors_o, v_errors_o)
    get_anchor = go.start(anchor_o, v_anchor_o)
    get_table = go.start(table, v_table)
    get_users.wait()
    get_relation.wait()
    v_anchor[...] = dot(v_users[...], v_relation[...], 1, 0).astype(narrow)
    get_items.wait()
    get_labels.wait()
    for at in tiles(v_items.shape[0]):
        scores = dot(v_anchor[...], v_items[at, :], 1, 1)
        v_errors[:, at] = errors_of(scores, v_labels[:, at])
    go.send(v_errors, errors_p)
    get_mapped.wait()
    v_grad[...] = dot(v_errors[...], v_mapped[...], 1, 0).astype(narrow)
    go.send(v_grad, grad_b)
    get_errors.wait()
    get_anchor.wait()
    get_table.wait()
    for at in tiles(v_items.shape[0]):
        grads = dot(v_errors_o[:, at], v_anchor_o[...], 0, 0) + dot(v_errors[:, at], v_anchor[...], 0, 0)
        new, accum = adagrad_rows(v_table[at, :], as_column(sums[:, at]), grads)
        v_next[at, :] = new.astype(narrow)
        sums_next[:, at] = as_line(accum)
        go.send(v_next.at[at, :], items_next.at[at, :])
    go.finish()


def first_peer(place, users, relation, items_b, targets, mapped, errors_o, anchor_o, table, sums, turn):
    n, d = users.shape
    m = table.shape[0]
    line = pl.BlockSpec(memory_space=pltpu.VMEM)
    return manual(
        functools.partial(peer_body, turn=turn),
        [pl.BlockSpec(memory_space=pltpu.SMEM), line] + [anywhere()] * 8,
        [anywhere()] * 3 + [line],
        [shape(narrow, n, m), shape(narrow, n, d), shape(narrow, m, d), shape(single, 1, m)],
        [
            pltpu.VMEM((n, d), narrow),
            pltpu.VMEM((d, d), narrow),
            pltpu.VMEM((m, d), narrow),
            pltpu.VMEM((n, m), narrow),
            pltpu.VMEM((m, d), narrow),
            pltpu.VMEM((n, m), narrow),
            pltpu.VMEM((n, d), narrow),
            pltpu.VMEM((m, d), single),
            pltpu.VMEM((n, d), narrow),
            pltpu.VMEM((n, m), narrow),
            pltpu.VMEM((n, d), narrow),
            pltpu.VMEM((m, d), narrow),
        ],
        10 + m // TILE,
        2 * n * d * d + 8 * n * m * d,
    )(place, sums, users, relation, items_b, targets, mapped, errors_o, anchor_o, table)


def ahead_body(table, grad, more, sums, relation, turned, anchor):
    new, _ = adagrad_rows(wide(table[...]), as_column(sums[...]), wide(grad[...]) + wide(more[...]))
    new = new.astype(narrow)
    turned[...] = jnp.transpose(new)
    anchor[...] = dot(new, relation[...], 1, 0).astype(narrow)


def ahead(table, grad, more, sums, relation):
    n, d = table.shape
    tile = pl.BlockSpec((TILE, d), lambda j: (j, 0))
    return call(
        ahead_body,
        (n // TILE,),
        [tile, tile, tile, pl.BlockSpec((1, TILE), lambda j: (0, j)), whole(d, d)],
        [pl.BlockSpec((d, TILE), lambda j: (0, j)), tile],
        [shape(narrow, d, n), shape(narrow, n, d)],
        [],
        2 * n * d * d,
    )(table, grad, more, sums, relation)


def term_body(users_o, users_p, errors_o, errors_p, items, term, turned_o, turned_p):
    j = pl.program_id(0)

    @pl.when(j == 0)
    def _():
        turned_o[...] = jnp.transpose(users_o[...])
        turned_p[...] = jnp.transpose(users_p[...])

    crossed = dot(turned_o[...], errors_o[...], 1, 0) + dot(turned_p[...], errors_p[...], 1, 0)
    part = dot(crossed.astype(narrow), items[...], 1, 0)

    @pl.when(j == 0)
    def _():
        term[...] = part

    @pl.when(j > 0)
    def _():
        term[...] += part


def first_term(users_o, users_p, errors_o, errors_p, items):
    n, d = users_o.shape
    m = items.shape[0]
    tile = pl.BlockSpec((TILE, d), lambda j: (j, 0))
    side = pl.BlockSpec((n, TILE), lambda j: (0, j))
    return call(
        term_body,
        (m // TILE,),
        [whole(n, d), whole(n, d), side, side, tile],
        whole(d, d),
        shape(single, d, d),
        [pltpu.VMEM((d, n), narrow), pltpu.VMEM((d, n), narrow)],
        4 * n * m * d + 2 * m * d * d,
    )(users_o, users_p, errors_o, errors_p, items)


def second_body(
    place, sums, item_sums, table, grad, more, relation, anchor_p, turned_p, items, targets, term,
    users_next, errors, term_keep, term_give, next_a, next_b, sums_next, item_sums_next,
    v_table, v_grad, v_more, v_relation, v_anchor, v_turned, v_items, v_labels, v_term,
    v_users, v_errors, v_crossed, v_next, sems,
    turn,
):
    go = Copies(sems)
    n, d = table.shape
    m = items.shape[0]
    get_more = go.start(more, v_more)
    get_table = go.start(table, v_table)
    get_grad = go.start(grad, v_grad)
    get_relation = go.start(relation, v_relation)
    get_anchor = go.start(anchor_p, v_anchor.at[n:, :])
    get_items, get_labels = [], []
    for at in tiles(m):
        get_items.append(go.start(items.at[at, :], v_items.at[at, :]))
        for half, first in ((0, place[0]), (1, 1 - place[0])):
            rows = pl.ds(pl.multiple_of(first * n, n), n)
            get_labels.append(
                go.start(targets.at[turn, rows, at], v_labels.at[half * n : half * n + n, at])
            )
    get_turned = go.start(turned_p, v_turned.at[:, n:])
    get_term = go.start(term, v_term)
    get_more.wait()
    get_table.wait()
    get_grad.wait()
    for at in tiles(n):
        new, accum = adagrad_rows(
            v_table[at, :], as_column(sums[:, at]), v_grad[at, :] + wide(v_more[at, :])
        )
        v_users[at, :] = new
        sums_next[:, at] = as_line(accum)
        v_turned[:, at] = jnp.transpose(new.astype(narrow))
    go.send(v_users, users_next)
    get_relation.wait()
    v_anchor[:n, :] = dot(v_users[...].astype(narrow), v_relation[...], 1, 0).astype(narrow)
    get_anchor.wait()
    for k, at in enumerate(tiles(m)):
        get_items[k].wait()
        get_labels[2 * k].wait()
        get_labels[2 * k + 1].wait()
        scores = dot(v_anchor[...], v_items[at, :], 1, 1)
        v_errors[:, at] = errors_of(scores, v_labels[:, at])
        go.send(v_errors.at[:, at], errors.at[:, at])
    get_turned.wait()
    get_term.wait()
    for at in tiles(d):
        v_crossed[at, :] = dot(v_turned[at, :], v_errors[...], 1, 0).astype(narrow)
        v_term[at, :] += dot(v_crossed[at, :], v_items[...], 1, 0)
    half = d // 2
    keep = pl.multiple_of(place[1] * half, half)
    give = pl.multiple_of((1 - place[1]) * half, half)
    go.send(v_term.at[pl.ds(give, half), :], term_give)
    go.send(v_term.at[pl.ds(keep, half), :], term_keep)
    for at in tiles(m):
        grads = dot(v_errors[:, at], v_anchor[...], 0, 0)
        new, accum = adagrad_rows(wide(v_items[at, :]), as_column(item_sums[:, at]), grads)
        v_next[at, :] = new.astype(narrow)
        item_sums_next[:, at] = as_line(accum)
        if at.start < m // 2:
            go.send(v_next.at[at, :], next_a.at[at, :])
        else:
            go.send(v_next.at[at, :], next_b.at[at.start - m // 2 : at.stop - m // 2, :])
    go.finish()


def second(place, table, grad, more, sums, relation, anchor_p, turned_p, items, item_sums, targets, term, turn):
    n, d = table.shape
    m = items.shape[0]
    line = pl.BlockSpec(memory_space=pltpu.VMEM)
    return manual(
        functools.partial(second_body, turn=turn),
        [pl.BlockSpec(memory_space=pltpu.SMEM), line, line] + [anywhere()] * 9,
        [anywhere()] * 6 + [line, line],
        [
            shape(single, n, d),
            shape(narrow, 2 * n, m),
            shape(single, d // 2, d),
            shape(single, d // 2, d),
            shape(narrow, m // 2, d),
            shape(narrow, m // 2, d),
            shape(single, 1, n),
            shape(single, 1, m),
        ],
        [
            pltpu.VMEM((n, d), single),
            pltpu.VMEM((n, d), single),
            pltpu.VMEM((n, d), narrow),
            pltpu.VMEM((d, d), narrow),
            pltpu.VMEM((2 * n, d), narrow),
            pltpu.VMEM((d, 2 * n), narrow),
            pltpu.VMEM((m, d), narrow),
            pltpu.VMEM((2 * n, m), narrow),
            pltpu.VMEM((d, d), single),
            pltpu.VMEM((n, d), single),
            pltpu.VMEM((2 * n, m), narrow),
            pltpu.VMEM((d, m), narrow),
            pltpu.VMEM((m, d), narrow),
        ],
        10 + 5 * (m // TILE),
        2 * n * d * d + 12 * n * m * d + 2 * m * d * d,
    )(place, sums, item_sums, table, grad, more, relation, anchor_p, turned_p, items, targets, term)


def grads_body(errors, items, relation, grad_o, grad_p,
               v_errors, v_items, v_relation, v_mapped, v_grad_o, v_grad_p, sems):
    go = Copies(sems)
    n = grad_o.shape[0]
    get_items = go.start(items, v_items)
    get_relation = go.start(relation, v_relation)
    rows = tiles(2 * n)
    order = rows[len(rows) // 2 :] + rows[: len(rows) // 2]
    get = [go.start(errors.at[at, :], v_errors.at[at, :]) for at in order]
    get_items.wait()
    get_relation.wait()
    v_mapped[...] = dot(v_items[...], v_relation[...], 1, 1).astype(narrow)
    for at, copy in zip(order, get):
        copy.wait()
        part = dot(v_errors[at, :], v_mapped[...], 1, 0)
        if at.start >= n:
            there = slice(at.start - n, at.stop - n)
            v_grad_p[there, :] = part.astype(narrow)
            go.send(v_grad_p.at[there, :], grad_p.at[there, :])
        else:
            v_grad_o[at, :] = part
            go.send(v_grad_o.at[at, :], grad_o.at[at, :])
    go.finish()


def second_grads(errors, items, relation):
    n = errors.shape[0] // 2
    m, d = items.shape
    return manual(
        grads_body,
        [anywhere()] * 3,
        [anywhere()] * 2,
        [shape(single, n, d), shape(narrow, n, d)],
        [
            pltpu.VMEM((2 * n, m), narrow),
            pltpu.VMEM((m, d), narrow),
            pltpu.VMEM((d, d), narrow),
            pltpu.VMEM((m, d), narrow),
            pltpu.VMEM((n, d), single),
            pltpu.VMEM((n, d), narrow),
        ],
        2 + 4 * (n // TILE),
        4 * n * m * d + 2 * m * d * d,
    )(errors, items, relation)


def users_body(table, grad, more, sums, table_next, sums_next):
    new, accum = adagrad_rows(table[...], as_column(sums[...]), grad[...] + wide(more[...]))
    table_next[...] = new
    sums_next[...] = as_line(accum)


def update_users(table, grad, more, sums):
    n, d = table.shape
    tile = pl.BlockSpec((TILE, d), lambda j: (j, 0))
    line = pl.BlockSpec((1, TILE), lambda j: (0, j))
    return call(
        users_body,
        (n // TILE,),
        [tile, tile, tile, line],
        [tile, line],
        [shape(single, n, d), shape(single, 1, n)],
        [],
        4 * n * d,
    )(table, grad, more, sums)


def pick(parts, key):
    n = len(parts)
    level = 1
    while level < n:
        bit = (key // level) % 2 == 1
        parts = [jnp.where(bit, parts[k ^ level], parts[k]) for k in range(n)]
        level *= 2
    return jnp.concatenate(parts, axis=0)


def relation_total(keep, give):
    blocks = lax.axis_size("blk")
    b, r = lax.axis_index("blk"), lax.axis_index("rel")
    core = b % 2
    half = keep.shape[0]
    p = keep + exchange(give, 1, 0)
    key = r + 2 * ((b // 2) % 2)
    part = half // 4
    total = lax.dynamic_slice_in_dim(p, key * part, part)
    got = []
    for k in (3, 1, 2):
        piece = lax.dynamic_slice_in_dim(p, (key ^ k) * part, part).astype(narrow)
        got.append(wide(exchange(piece, 2 * (k // 2), k % 2)))
    total = total + (got[0] + (got[1] + got[2]))
    flip = 4
    while blocks // flip > 8:
        sent = total.astype(narrow)
        total = wide(sent) + wide(exchange(sent, flip, 0))
        flip *= 2
    sent = total.astype(narrow)
    parts = [wide(sent)]
    for k in range(1, blocks // flip):
        parts.append(wide(exchange(sent, flip * k, 0)))
    while len(parts) > 1:
        parts = [parts[i] + parts[i + 1] for i in range(0, len(parts), 2)]
    sent = parts[0].astype(narrow)
    parts = [sent] + [exchange(sent, 2 * (k // 2), k % 2) for k in (1, 2, 3)]
    p = pick(parts, key)
    return pick([p, exchange(p, 1, 0)], core)


def step(user_table, user_accum, item_table, item_accum, relation, relation_accum, targets):
    blocks = lax.axis_size("blk")
    rounds = targets.shape[0]
    assert rounds == 2 and lax.axis_size("rel") == 2
    place = jnp.stack([lax.axis_index("rel"), lax.axis_index("blk") % 2]).astype(jnp.int32)
    sums_o, item_sums = user_accum[None, :], item_accum[None, :]

    mine = user_table.astype(narrow)
    theirs = swap(mine)
    items, mapped, anchor_o, errors_o, grad_o, grad_ob = first_own(
        place[:1], mine, item_table, relation, targets, 0
    )
    more_p = swap(grad_ob)
    sums_p = swap(sums_o)
    errors_p, grad_pb, items_next, item_sums = first_peer(
        place, theirs, relation, items, targets, mapped, errors_o, anchor_o, item_table, item_sums, 0
    )
    more_o = swap(grad_pb)
    items_next = from_behind(items_next)
    item_sums = from_behind(item_sums)
    term = first_term(mine, theirs, errors_o, errors_p, items)
    turned_p, anchor_p = ahead(theirs, grad_pb, more_p, sums_p, relation)

    users, errors, keep, give, *chunks, sums_o, item_sums = second(
        place, user_table, grad_o, more_o, sums_o, relation, anchor_p, turned_p,
        items_next, item_sums, targets, term, 1,
    )
    grad_o, grad_pb = second_grads(errors, items_next, relation)
    more_o = swap(grad_pb)
    chunks = [from_behind(chunk) for chunk in chunks]
    item_sums = from_behind(item_sums)
    users, sums_o = update_users(users, grad_o, more_o, sums_o)

    total = wide(relation_total(keep, give))
    mean_grad = total / (blocks * rounds)
    accum_next = relation_accum + jnp.mean(mean_grad * mean_grad, axis=1)
    relation_step = mean_grad * lax.rsqrt(accum_next + epsilon)[:, None]
    items_last = jnp.concatenate([wide(chunk) for chunk in chunks], axis=0)
    return (users, sums_o[0], items_last, item_sums[0], relation_step, accum_next)


def solution(mesh):
    rows = P(("blk", "rel"), None)
    line = P(("blk", "rel"))
    return jax.shard_map(
        step,
        mesh=mesh,
        in_specs=(rows, line, rows, line, P(), P(), P(None, "blk", "rel")),
        out_specs=(rows, line, rows, line, P(), P()),
        check_vma=False,
    )
```

profile of v0, /device:TPU:0, one launch (start us, length us, event | category | flops | bytes accessed | tf_op | source)
XLA Modules:
  0.0 127.2 jit_solution(17926583112198893783)
XLA Ops:
  0.6 2.1 %convert_element_type.44.users.users_o = bf16[512,512]{1,0:T(8,128)(2,1)} convert(f32[512,512]{1,0:T(8,128)} %table.3) | non-fusion elementwise | flops 262144 | bytes 1572864 | tf_op jit(solution)/shard_map/convert_element_type | solution.py:530
  2.7 3.0 %collective-permute-start = (bf16[512,512]{1,0:T(8,128)(2,1)}, bf16[512,512]{1,0:T(8,128)(2,1)S(1)}, u32[]{:S(2)}, u32[]{:S(2)}) collective-permute-start(bf16[512,512]{1,0:T(8,128)(2,1)} %convert_element_type.44.users.users_o), channel_id=1, source_target_pairs={{0,1},{1,0},{2,3},{3,2},{4,5},{5,4},{6,7},{7,6},{8,9},{9,8},{10,11... | collective-permute-start | bytes 1572872 | tf_op jit(solution)/shard_map/ppermute | solution.py:23
  6.3 7.9 %shard_map.118 = (bf16[1024,512]{1,0:T(8,128)(2,1)}, bf16[1024,512]{1,0:T(8,128)(2,1)}, bf16[512,512]{1,0:T(8,128)(2,1)}, bf16[512,1024]{1,0:T(8,128)(2,1)}, f32...) custom-call(s32[1]{0:T(128)} %bitcast.place, bf16[512,512]{1,0:T(8,128)(2,1)} %convert_element_type.44.users.users_o, ...), custom_call_target="tpu_custom_call" | custom-call | flops 1879048192 | bytes 4194304 | tf_op jit(solution)/shard_map/pallas_call | solution.py:156
  14.2 3.7 %collective-permute-done.users.table.users_p = bf16[512,512]{1,0:T(8,128)(2,1)S(1)} collective-permute-done((bf16[512,512]{1,0:T(8,128)(2,1)}, bf16[512,512]{1,0:T(8,128)(2,1)S(1)}, u32[]{:S(2)}, u32[]{:S(2)}) %collective-permute-start) | collective-permute-done | bytes 524320 | tf_op jit(solution)/shard_map/ppermute | solution.py:23
  18.6 7.7 %shard_map.119 = (bf16[512,1024]{1,0:T(8,128)(2,1)}, bf16[512,512]{1,0:T(8,128)(2,1)}, bf16[1024,512]{1,0:T(8,128)(2,1)}, f32[1,1024]{1,0:T(1,128)}) custom-call(s32[2]{0:T(128)} %pad_add_fusion.place, f32[1,1024]{1,0:T(1,128)} %bitcast.6, bf16[512,512]{1,0:T(8,128)(2,1)} %copy-done, bf16[512,512]{1,0:T(8,128)(2,1)} %relation.9, ...), custom_call_target="tpu_custom_call" | custom-call | flops 2415919104 | bytes 4194304 | tf_op jit(solution)/shard_map/pallas_call | solution.py:228
  26.4 1.8 %collective-permute-start.3 = (bf16[512,512]{1,0:T(8,128)(2,1)}, bf16[512,512]{1,0:T(8,128)(2,1)S(1)}, u32[]{:S(2)}, u32[]{:S(2)}) collective-permute-start(bf16[512,512]{1,0:T(8,128)(2,1)} %get-tuple-element.37), channel_id=1, source_target_pairs={{0,1},{1,0},{2,3},{3,2},{4,5},{5,4},{6,7},{7,6},{8,9},{9,8},{10,11... | collective-permute-start | bytes 1572872 | tf_op jit(solution)/shard_map/ppermute | solution.py:23
  28.5 1.7 %collective-permute-start.4 = (f32[1,512]{1,0:T(1,128)S(1)}, f32[1,512]{1,0:T(1,128)S(1)}, u32[]{:S(2)}, u32[]{:S(2)}) collective-permute-start(f32[1,512]{1,0:T(1,128)S(1)} %bitcast.9), channel_id=1, source_target_pairs={{0,1},{1,0},{2,3},{3,2},{4,5},{5,4},{6,7},{7,6},{8,9},{9,8},{10,11... | collective-permute-start | bytes 6152 | tf_op jit(solution)/shard_map/ppermute | solution.py:23
  30.9 6.7 %shard_map.121.term = f32[512,512]{1,0:T(8,128)} custom-call(bf16[512,512]{1,0:T(8,128)(2,1)} %convert_element_type.44.users.users_o, bf16[512,512]{1,0:T(8,128)(2,1)} %copy-done, bf16[512,1024]{1,0:T(8,128)(2,1)} %get-tuple-element.32.errors_o, bf16[512,1024]{1,0:T(8,128)(2,1)} %get-tuple-element.41.errors_p, bf16[1024,512]{1,0:T(8,128)(2,1)} %get-tuple-element.30.items_b.items), custom_call_target="tpu_custom_call" | custom-call | flops 1610612736 | bytes 4194304 | tf_op jit(solution)/shard_map/pallas_call | solution.py:298
  37.6 14.3 %collective-permute-done.4.sums = f32[1,512]{1,0:T(1,128)S(1)} collective-permute-done((f32[1,512]{1,0:T(1,128)S(1)}, f32[1,512]{1,0:T(1,128)S(1)}, u32[]{:S(2)}, u32[]{:S(2)}) %collective-permute-start.4) | collective-permute-done | bytes 2080 | tf_op jit(solution)/shard_map/ppermute | solution.py:23
  53.3 3.4 %shard_map.120 = (bf16[512,512]{1,0:T(8,128)(2,1)}, bf16[512,512]{1,0:T(8,128)(2,1)}) custom-call(bf16[512,512]{1,0:T(8,128)(2,1)} %copy-done, bf16[512,512]{1,0:T(8,128)(2,1)} %get-tuple-element.36.grad, bf16[512,512]{1,0:T(8,128)(2,1)} %copy-done.1, f32[1,512]{1,0:T(1,128)} %copy-done.2, bf16[512,512]{1,0:T(8,128)(2,1)} %relation.9), custom_call_target="tpu_custom_call" | custom-call | flops 268435456 | bytes 4194304 | tf_op jit(solution)/shard_map/pallas_call | solution.py:262
  57.3 11.4 %shard_map.122 = (f32[512,512]{1,0:T(8,128)}, bf16[1024,1024]{1,0:T(8,128)(2,1)}, f32[256,512]{1,0:T(8,128)}, f32[256,512]{1,0:T(8,128)}, bf16[512,512]{1,0:T(8,...) custom-call(s32[2]{0:T(128)} %pad_add_fusion.place, f32[1,512]{1,0:T(1,128)} %bitcast.8, ...), custom_call_target="tpu_custom_call" | custom-call | flops 4026531840 | bytes 4194304 | tf_op jit(solution)/shard_map/pallas_call | solution.py:381
  69.5 1.7 %collective-permute-done.10 = f32[256,512]{1,0:T(8,128)S(1)} collective-permute-done((f32[256,512]{1,0:T(8,128)}, f32[256,512]{1,0:T(8,128)S(1)}, u32[]{:S(2)}, u32[]{:S(2)}) %collective-permute-start.10) | collective-permute-done | bytes 524320 | tf_op jit(solution)/shard_map/ppermute | solution.py:23
  72.4 2.8 %collective-permute-start.11 = (bf16[64,512]{1,0:T(8,128)(2,1)S(1)}, bf16[64,512]{1,0:T(8,128)(2,1)S(1)}, u32[]{:S(2)}, u32[]{:S(2)}) collective-permute-start(bf16[64,512]{1,0:T(8,128)(2,1)S(1)} %get-tuple-element.58), channel_id=1, source_target_pairs={{0,5},{1,4},{2,7},{3,6},{4,1},{5,0},{6,3},{7,2},{8,13},{9,12},{10,... | collective-permute-start | bytes 196616 | tf_op jit(solution)/shard_map/ppermute | solution.py:23
  76.0 1.9 %collective-permute-done.11 = bf16[64,512]{1,0:T(8,128)(2,1)S(1)} collective-permute-done((bf16[64,512]{1,0:T(8,128)(2,1)S(1)}, bf16[64,512]{1,0:T(8,128)(2,1)S(1)}, u32[]{:S(2)}, u32[]{:S(2)}) %collective-permute-start.11) | collective-permute-done | bytes 65568 | tf_op jit(solution)/shard_map/ppermute | solution.py:23
  80.0 1.6 %collective-permute-start.14 = (bf16[64,512]{1,0:T(8,128)(2,1)S(1)}, bf16[64,512]{1,0:T(8,128)(2,1)S(1)}, u32[]{:S(2)}, u32[]{:S(2)}) collective-permute-start(bf16[64,512]{1,0:T(8,128)(2,1)S(1)} %add_convert_fusion.1), channel_id=1, source_target_pairs={{0,8},{1,9},{2,10},{3,11},{4,12},{5,13},{6,14},{7,15},{8,0},{9,1},... | collective-permute-start | bytes 196616 | tf_op jit(solution)/shard_map/ppermute | solution.py:23
  81.7 2.1 %collective-permute-start.15 = (bf16[64,512]{1,0:T(8,128)(2,1)S(1)}, bf16[64,512]{1,0:T(8,128)(2,1)S(1)}, u32[]{:S(2)}, u32[]{:S(2)}) collective-permute-start(bf16[64,512]{1,0:T(8,128)(2,1)S(1)} %add_convert_fusion.1), channel_id=1, source_target_pairs={{0,16},{1,17},{2,18},{3,19},{4,20},{5,21},{6,22},{7,23},{8,24},{9,... | collective-permute-start | bytes 196616 | tf_op jit(solution)/shard_map/ppermute | solution.py:23
  85.0 3.2 %collective-permute-done.15 = bf16[64,512]{1,0:T(8,128)(2,1)S(1)} collective-permute-done((bf16[64,512]{1,0:T(8,128)(2,1)S(1)}, bf16[64,512]{1,0:T(8,128)(2,1)S(1)}, u32[]{:S(2)}, u32[]{:S(2)}) %collective-permute-start.15) | collective-permute-done | bytes 65568 | tf_op jit(solution)/shard_map/ppermute | solution.py:23
  89.9 2.3 %collective-permute-start.17 = (bf16[64,512]{1,0:T(8,128)(2,1)S(1)}, bf16[64,512]{1,0:T(8,128)(2,1)S(1)}, u32[]{:S(2)}, u32[]{:S(2)}) collective-permute-start(bf16[64,512]{1,0:T(8,128)(2,1)S(1)} %add_convert_fusion), channel_id=1, source_target_pairs={{0,5},{1,4},{2,7},{3,6},{4,1},{5,0},{6,3},{7,2},{8,13},{9,12},{10,... | collective-permute-start | bytes 196616 | tf_op jit(solution)/shard_map/ppermute | solution.py:23
  92.1 4.7 %shard_map.123 = (f32[512,512]{1,0:T(8,128)}, bf16[512,512]{1,0:T(8,128)(2,1)}) custom-call(bf16[1024,1024]{1,0:T(8,128)(2,1)} %get-tuple-element.43.errors, bf16[1024,512]{1,0:T(8,128)(2,1)} %collective-permute-done.5.items, bf16[512,512]{1,0:T(8,128)(2,1)} %relation.9), custom_call_target="tpu_custom_call" | custom-call | flops 1610612736 | bytes 4194304 | tf_op jit(solution)/shard_map/pallas_call | solution.py:443
  102.6 7.2 %collective-permute-done.19 = bf16[64,512]{1,0:T(8,128)(2,1)S(1)} collective-permute-done((bf16[64,512]{1,0:T(8,128)(2,1)S(1)}, bf16[64,512]{1,0:T(8,128)(2,1)S(1)}, u32[]{:S(2)}, u32[]{:S(2)}) %collective-permute-start.19) | collective-permute-done | bytes 65568 | tf_op jit(solution)/shard_map/ppermute | solution.py:23
  110.6 1.9 %collective-permute-start.20 = (bf16[256,512]{1,0:T(8,128)(2,1)}, bf16[256,512]{1,0:T(8,128)(2,1)}, u32[]{:S(2)}, u32[]{:S(2)}) collective-permute-start(bf16[256,512]{1,0:T(8,128)(2,1)} %pad_maximum_fusion.1), channel_id=1, source_target_pairs={{0,2},{1,3},{2,0},{3,1},{4,6},{5,7},{6,4},{7,5},{8,10},{9,11},{10,... | collective-permute-start | bytes 786440 | tf_op jit(solution)/shard_map/ppermute | solution.py:23
  112.5 5.7 %collective-permute-done.9 = f32[1,1024]{1,0:T(1,128)S(1)} collective-permute-done((f32[1,1024]{1,0:T(1,128)S(1)}, f32[1,1024]{1,0:T(1,128)S(1)}, u32[]{:S(2)}, u32[]{:S(2)}) %collective-permute-start.9) | collective-permute-done | bytes 4128 | tf_op jit(solution)/shard_map/ppermute | solution.py:32
  118.2 2.8 %shard_map.124 = (f32[512,512]{1,0:T(8,128)}, f32[1,512]{1,0:T(1,128)}) custom-call(f32[512,512]{1,0:T(8,128)} %get-tuple-element.42.table, f32[512,512]{1,0:T(8,128)} %get-tuple-element.44.grad, bf16[512,512]{1,0:T(8,128)(2,1)} %collective-permute-done.6.more, f32[1,512]{1,0:T(1,128)} %get-tuple-element.46.sums), custom_call_target="tpu_custom_call" | custom-call | flops 1048576 | bytes 4194304 | tf_op jit(solution)/shard_map/pallas_call | solution.py:471
  121.0 2.7 %maximum_convert_fusion = f32[1024,512]{1,0:T(8,128)} fusion(bf16[512,512]{1,0:T(8,128)(2,1)} %collective-permute-done.8, bf16[512,512]{1,0:T(8,128)(2,1)S(1)} %collective-permute-done.7), kind=kLoop, calls=%fused_computation.4 | loop fusion | flops 2097152 | bytes 3145728 | tf_op jit(solution)/shard_map/concatenate | solution.py:560
  (53 shorter events, 22.2 us)
Async XLA Ops:
  2.7 15.1 %collective-permute-start = (bf16[512,512]{1,0:T(8,128)(2,1)}, bf16[512,512]{1,0:T(8,128)(2,1)S(1)}, u32[]{:S(2)}, u32[]{:S(2)}) collective-permute-start(bf16[512,512]{1,0:T(8,128)(2,1)} %convert_element_type.44.users.users_o), channel_id=1, source_target_pairs={{0,1},{1,0},{2,3},{3,2},{4,5},{5,4},{6,7},{7,6},{8,9},{9,8},{10,11... | collective-permute-start | bytes 1572872 | tf_op jit(solution)/shard_map/ppermute | solution.py:23
  18.6 9.8 %copy-start.6 = (f32[512]{0:T(512)S(1)}, f32[512]{0:T(512)}, u32[]{:S(2)}) copy-start(f32[512]{0:T(512)} %param.8) | copy-start | bytes 6148
  26.3 30.4 %collective-permute-start.5 = (bf16[1024,512]{1,0:T(8,128)(2,1)}, bf16[1024,512]{1,0:T(8,128)(2,1)}, u32[]{:S(2)}, u32[]{:S(2)}) collective-permute-start(bf16[1024,512]{1,0:T(8,128)(2,1)} %get-tuple-element.40), channel_id=1, source_target_pairs={{0,2},{2,4},{4,6},{6,8},{8,10},{10,12},{12,14},{14,16},{16,18},{18... | collective-permute-start | bytes 3145736 | tf_op jit(solution)/shard_map/ppermute | solution.py:32
  26.4 25.6 %collective-permute-start.3 = (bf16[512,512]{1,0:T(8,128)(2,1)}, bf16[512,512]{1,0:T(8,128)(2,1)S(1)}, u32[]{:S(2)}, u32[]{:S(2)}) collective-permute-start(bf16[512,512]{1,0:T(8,128)(2,1)} %get-tuple-element.37), channel_id=1, source_target_pairs={{0,1},{1,0},{2,3},{3,2},{4,5},{5,4},{6,7},{7,6},{8,9},{9,8},{10,11... | collective-permute-start | bytes 1572872 | tf_op jit(solution)/shard_map/ppermute | solution.py:23
  28.2 28.6 %collective-permute-start.2 = (bf16[512,512]{1,0:T(8,128)(2,1)}, bf16[512,512]{1,0:T(8,128)(2,1)}, u32[]{:S(2)}, u32[]{:S(2)}) collective-permute-start(bf16[512,512]{1,0:T(8,128)(2,1)} %get-tuple-element.36.grad), channel_id=1, source_target_pairs={{0,1},{1,0},{2,3},{3,2},{4,5},{5,4},{6,7},{7,6},{8,9},{9,8},{10,11... | collective-permute-start | bytes 1572872 | tf_op jit(solution)/shard_map/ppermute | solution.py:23
  28.5 23.5 %collective-permute-start.4 = (f32[1,512]{1,0:T(1,128)S(1)}, f32[1,512]{1,0:T(1,128)S(1)}, u32[]{:S(2)}, u32[]{:S(2)}) collective-permute-start(f32[1,512]{1,0:T(1,128)S(1)} %bitcast.9), channel_id=1, source_target_pairs={{0,1},{1,0},{2,3},{3,2},{4,5},{5,4},{6,7},{7,6},{8,9},{9,8},{10,11... | collective-permute-start | bytes 6152 | tf_op jit(solution)/shard_map/ppermute | solution.py:23
  30.2 26.5 %collective-permute-start.1 = (f32[1,1024]{1,0:T(1,128)}, f32[1,1024]{1,0:T(1,128)S(1)}, u32[]{:S(2)}, u32[]{:S(2)}) collective-permute-start(f32[1,1024]{1,0:T(1,128)} %get-tuple-element.34), channel_id=1, source_target_pairs={{0,2},{2,4},{4,6},{6,8},{8,10},{10,12},{12,14},{14,16},{16,18},{18... | collective-permute-start | bytes 12296 | tf_op jit(solution)/shard_map/ppermute | solution.py:32
  68.8 2.5 %collective-permute-start.10 = (f32[256,512]{1,0:T(8,128)}, f32[256,512]{1,0:T(8,128)S(1)}, u32[]{:S(2)}, u32[]{:S(2)}) collective-permute-start(f32[256,512]{1,0:T(8,128)} %get-tuple-element.53), channel_id=1, source_target_pairs={{0,2},{1,3},{2,0},{3,1},{4,6},{5,7},{6,4},{7,5},{8,10},{9,11},{10,... | collective-permute-start | bytes 1572872 | tf_op jit(solution)/shard_map/ppermute | solution.py:23
  72.4 5.4 %collective-permute-start.11 = (bf16[64,512]{1,0:T(8,128)(2,1)S(1)}, bf16[64,512]{1,0:T(8,128)(2,1)S(1)}, u32[]{:S(2)}, u32[]{:S(2)}) collective-permute-start(bf16[64,512]{1,0:T(8,128)(2,1)S(1)} %get-tuple-element.58), channel_id=1, source_target_pairs={{0,5},{1,4},{2,7},{3,6},{4,1},{5,0},{6,3},{7,2},{8,13},{9,12},{10,... | collective-permute-start | bytes 196616 | tf_op jit(solution)/shard_map/ppermute | solution.py:23
  75.2 4.3 %collective-permute-start.12 = (bf16[64,512]{1,0:T(8,128)(2,1)S(1)}, bf16[64,512]{1,0:T(8,128)(2,1)S(1)}, u32[]{:S(2)}, u32[]{:S(2)}) collective-permute-start(bf16[64,512]{1,0:T(8,128)(2,1)S(1)} %get-tuple-element.60), channel_id=1, source_target_pairs={{0,1},{1,0},{2,3},{3,2},{4,5},{5,4},{6,7},{7,6},{8,9},{9,8},{10,11... | collective-permute-start | bytes 196616 | tf_op jit(solution)/shard_map/ppermute | solution.py:23
  75.7 4.3 %collective-permute-start.13 = (bf16[64,512]{1,0:T(8,128)(2,1)S(1)}, bf16[64,512]{1,0:T(8,128)(2,1)S(1)}, u32[]{:S(2)}, u32[]{:S(2)}) collective-permute-start(bf16[64,512]{1,0:T(8,128)(2,1)S(1)} %get-tuple-element.59), channel_id=1, source_target_pairs={{0,4},{1,5},{2,6},{3,7},{4,0},{5,1},{6,2},{7,3},{8,12},{9,13},{10,... | collective-permute-start | bytes 196616 | tf_op jit(solution)/shard_map/ppermute | solution.py:23
  80.0 5.0 %collective-permute-start.14 = (bf16[64,512]{1,0:T(8,128)(2,1)S(1)}, bf16[64,512]{1,0:T(8,128)(2,1)S(1)}, u32[]{:S(2)}, u32[]{:S(2)}) collective-permute-start(bf16[64,512]{1,0:T(8,128)(2,1)S(1)} %add_convert_fusion.1), channel_id=1, source_target_pairs={{0,8},{1,9},{2,10},{3,11},{4,12},{5,13},{6,14},{7,15},{8,0},{9,1},... | collective-permute-start | bytes 196616 | tf_op jit(solution)/shard_map/ppermute | solution.py:23
  81.7 6.6 %collective-permute-start.15 = (bf16[64,512]{1,0:T(8,128)(2,1)S(1)}, bf16[64,512]{1,0:T(8,128)(2,1)S(1)}, u32[]{:S(2)}, u32[]{:S(2)}) collective-permute-start(bf16[64,512]{1,0:T(8,128)(2,1)S(1)} %add_convert_fusion.1), channel_id=1, source_target_pairs={{0,16},{1,17},{2,18},{3,19},{4,20},{5,21},{6,22},{7,23},{8,24},{9,... | collective-permute-start | bytes 196616 | tf_op jit(solution)/shard_map/ppermute | solution.py:23
  83.8 6.1 %collective-permute-start.16 = (bf16[64,512]{1,0:T(8,128)(2,1)S(1)}, bf16[64,512]{1,0:T(8,128)(2,1)S(1)}, u32[]{:S(2)}, u32[]{:S(2)}) collective-permute-start(bf16[64,512]{1,0:T(8,128)(2,1)S(1)} %add_convert_fusion.1), channel_id=1, source_target_pairs={{0,24},{1,25},{2,26},{3,27},{4,28},{5,29},{6,30},{7,31},{8,16},{9,... | collective-permute-start | bytes 196616 | tf_op jit(solution)/shard_map/ppermute | solution.py:23
  89.9 10.0 %collective-permute-start.17 = (bf16[64,512]{1,0:T(8,128)(2,1)S(1)}, bf16[64,512]{1,0:T(8,128)(2,1)S(1)}, u32[]{:S(2)}, u32[]{:S(2)}) collective-permute-start(bf16[64,512]{1,0:T(8,128)(2,1)S(1)} %add_convert_fusion), channel_id=1, source_target_pairs={{0,5},{1,4},{2,7},{3,6},{4,1},{5,0},{6,3},{7,2},{8,13},{9,12},{10,... | collective-permute-start | bytes 196616 | tf_op jit(solution)/shard_map/ppermute | solution.py:23
  92.1 20.3 %copy-start.4 = (f32[1,1024]{1,0:T(1,128)S(1)}, f32[1,1024]{1,0:T(1,128)}, u32[]{:S(2)}) copy-start(f32[1,1024]{1,0:T(1,128)} %get-tuple-element.51) | copy-start | bytes 12292
  96.9 21.3 %collective-permute-start.6 = (bf16[512,512]{1,0:T(8,128)(2,1)}, bf16[512,512]{1,0:T(8,128)(2,1)}, u32[]{:S(2)}, u32[]{:S(2)}) collective-permute-start(bf16[512,512]{1,0:T(8,128)(2,1)} %get-tuple-element.45), channel_id=1, source_target_pairs={{0,1},{1,0},{2,3},{3,2},{4,5},{5,4},{6,7},{7,6},{8,9},{9,8},{10,11... | collective-permute-start | bytes 1572872 | tf_op jit(solution)/shard_map/ppermute | solution.py:23
  97.3 23.7 %collective-permute-start.7 = (bf16[512,512]{1,0:T(8,128)(2,1)}, bf16[512,512]{1,0:T(8,128)(2,1)S(1)}, u32[]{:S(2)}, u32[]{:S(2)}) collective-permute-start(bf16[512,512]{1,0:T(8,128)(2,1)} %get-tuple-element.49), channel_id=1, source_target_pairs={{0,2},{2,4},{4,6},{6,8},{8,10},{10,12},{12,14},{14,16},{16,18},{18... | collective-permute-start | bytes 1572872 | tf_op jit(solution)/shard_map/ppermute | solution.py:32
  97.3 23.7 %collective-permute-start.8 = (bf16[512,512]{1,0:T(8,128)(2,1)}, bf16[512,512]{1,0:T(8,128)(2,1)}, u32[]{:S(2)}, u32[]{:S(2)}) collective-permute-start(bf16[512,512]{1,0:T(8,128)(2,1)} %get-tuple-element.50), channel_id=1, source_target_pairs={{0,2},{2,4},{4,6},{6,8},{8,10},{10,12},{12,14},{14,16},{16,18},{18... | collective-permute-start | bytes 1572872 | tf_op jit(solution)/shard_map/ppermute | solution.py:32
  98.4 4.3 %collective-permute-start.18 = (bf16[64,512]{1,0:T(8,128)(2,1)S(1)}, bf16[64,512]{1,0:T(8,128)(2,1)S(1)}, u32[]{:S(2)}, u32[]{:S(2)}) collective-permute-start(bf16[64,512]{1,0:T(8,128)(2,1)S(1)} %add_convert_fusion), channel_id=1, source_target_pairs={{0,4},{1,5},{2,6},{3,7},{4,0},{5,1},{6,2},{7,3},{8,12},{9,13},{10,... | collective-permute-start | bytes 196616 | tf_op jit(solution)/shard_map/ppermute | solution.py:23
  99.8 10.0 %collective-permute-start.19 = (bf16[64,512]{1,0:T(8,128)(2,1)S(1)}, bf16[64,512]{1,0:T(8,128)(2,1)S(1)}, u32[]{:S(2)}, u32[]{:S(2)}) collective-permute-start(bf16[64,512]{1,0:T(8,128)(2,1)S(1)} %add_convert_fusion), channel_id=1, source_target_pairs={{0,1},{1,0},{2,3},{3,2},{4,5},{5,4},{6,7},{7,6},{8,9},{9,8},{10,11... | collective-permute-start | bytes 196616 | tf_op jit(solution)/shard_map/ppermute | solution.py:23
  110.6 13.1 %collective-permute-start.20 = (bf16[256,512]{1,0:T(8,128)(2,1)}, bf16[256,512]{1,0:T(8,128)(2,1)}, u32[]{:S(2)}, u32[]{:S(2)}) collective-permute-start(bf16[256,512]{1,0:T(8,128)(2,1)} %pad_maximum_fusion.1), channel_id=1, source_target_pairs={{0,2},{1,3},{2,0},{3,1},{4,6},{5,7},{6,4},{7,5},{8,10},{9,11},{10,... | collective-permute-start | bytes 786440 | tf_op jit(solution)/shard_map/ppermute | solution.py:23
  112.5 5.7 %collective-permute-start.9 = (f32[1,1024]{1,0:T(1,128)S(1)}, f32[1,1024]{1,0:T(1,128)S(1)}, u32[]{:S(2)}, u32[]{:S(2)}) collective-permute-start(f32[1,1024]{1,0:T(1,128)S(1)} %copy-done.4), channel_id=1, source_target_pairs={{0,2},{2,4},{4,6},{6,8},{8,10},{10,12},{12,14},{14,16},{16,18},{18... | collective-permute-start | bytes 12296 | tf_op jit(solution)/shard_map/ppermute | solution.py:32
  121.0 3.9 %copy-start.3 = (f32[512]{0:T(512)S(1)}, f32[512]{0:T(512)}, u32[]{:S(2)}) copy-start(f32[512]{0:T(512)} %param.12) | copy-start | bytes 6148
  (4 other events, 2.8 us)
where the time goes:
time: 128 us; the launch traced here: 127 us
  Pallas kernels  44.6 us (35%)
  waiting for transfers between devices  43.5 us (34%)
  starting transfers between devices  24.7 us (19%)
  other arithmetic  10.2 us (8%)
  local copies, waits for them, and re-layouts  3.36 us (3%)
    ppermute x16, waiting for transfers between devices, exchange(): return lax.ppermute(x, ('blk', 'rel'), pairs)  37.8 us
    ppermute x16, starting transfers between devices, exchange(): return lax.ppermute(x, ('blk', 'rel'), pairs)  22.9 us
    pallas_call x1, Pallas kernels, second(): manual(functools.partial(second_body, turn=turn), [pl.BlockSpec(memory_sp...  11.4 us
    pallas_call x1, Pallas kernels, first_own(): call(first_body, (m // TILE,), [whole(n, d), tile, whole(d, d), labels],...  7.87 us
    pallas_call x1, Pallas kernels, first_peer(): manual(functools.partial(peer_body, turn=turn), [pl.BlockSpec(memory_spac...  7.66 us
    pallas_call x1, Pallas kernels, first_term(): call(term_body, (m // TILE,), [whole(n, d), whole(n, d), side, side, tile...  6.71 us
    ppermute x5, waiting for transfers between devices, from_behind(): return lax.ppermute(x, 'blk', [(i, (i + 1) % peers) for i in range(peers)])  5.74 us
    pallas_call x1, Pallas kernels, second_grads(): manual(grads_body, [anywhere()] * 3, [anywhere()] * 2, [shape(single, n,...  4.74 us
  transfers between devices with their start and end apart: 21, of which 12 were waited for; matrix products, arithmetic and copies ran while one was open for 3% of the time, Pallas kernels for 20%

commit v1 on v0

--- a/solution.py
+++ b/solution.py
@@ -51,6 +51,10 @@
 def adagrad_rows(table, accum, grads):
     accum_next = accum + jnp.sum(grads * grads, axis=1, keepdims=True) * (1.0 / grads.shape[1])
     return table - grads * (learn_rate * lax.rsqrt(accum_next + epsilon)), accum_next
+
+
+def columns_into(scratch, line):
+    scratch[...] = jnp.transpose(jnp.broadcast_to(line, (8, line.shape[1])))
 
 
 def whole(*shape):
@@ -121,7 +125,7 @@
     return [slice(k * TILE, (k + 1) * TILE) for k in range(count // TILE)]
 
 
-def first_body(place, users, items, relation, labels, items_b, mapped, anchor, errors, grad, grad_b):
+def first_body(place, users, items, relation, labels, items_b, mapped, anchor, errors, grad_b, grad):
     j = pl.program_id(0)
 
     @pl.when(j == 0)
@@ -163,17 +167,15 @@
             whole(n, d),
             pl.BlockSpec((n, TILE), lambda j, place: (0, j)),
             whole(n, d),
-            whole(n, d),
         ],
         [
             shape(narrow, m, d),
             shape(narrow, m, d),
             shape(narrow, n, d),
             shape(narrow, n, m),
-            shape(single, n, d),
             shape(narrow, n, d),
         ],
-        [],
+        [pltpu.VMEM((n, d), single)],
         2 * n * d * d + 2 * m * d * d + 4 * n * m * d,
         prefetch=1,
     )(place, users, items, relation, targets)
@@ -181,25 +183,25 @@
 
 def peer_body(
     place, sums, users, relation, items_b, targets, mapped, errors_o, anchor_o, table,
-    errors_p, grad_b, items_next, sums_next,
-    v_users, v_relation, v_items, v_labels, v_mapped, v_errors_o, v_anchor_o, v_table,
-    v_anchor, v_errors, v_grad, v_next, sems,
+    users_b, errors_p, grad_b, items_next, sums_next,
+    v_relation, v_items, v_labels, v_mapped, v_errors_o, v_anchor_o, v_table,
+    v_anchor, v_errors, v_grad, v_next, v_sums, v_lines, sems,
     turn,
 ):
     go = Copies(sems)
     n = users.shape[0]
     peer_rows = pl.ds(pl.multiple_of((1 - place[0]) * n, n), n)
-    get_users = go.start(users, v_users)
     get_relation = go.start(relation, v_relation)
+    go.send(users, users_b)
     get_items = go.start(items_b, v_items)
     get_labels = go.start(targets.at[turn, peer_rows], v_labels)
     get_mapped = go.start(mapped, v_mapped)
     get_errors = go.start(errors_o, v_errors_o)
     get_anchor = go.start(anchor_o, v_anchor_o)
     get_table = go.start(table, v_table)
-    get_users.wait()
+    columns_into(v_sums, sums[...])
     get_relation.wait()
-    v_anchor[...] = dot(v_users[...], v_relation[...], 1, 0).astype(narrow)
+    v_anchor[...] = dot(users[...], v_relation[...], 1, 0).astype(narrow)
     get_items.wait()
     get_labels.wait()
     for at in tiles(v_items.shape[0]):
@@ -214,10 +216,12 @@
     get_table.wait()
     for at in tiles(v_items.shape[0]):
         grads = dot(v_errors_o[:, at], v_anchor_o[...], 0, 0) + dot(v_errors[:, at], v_anchor[...], 0, 0)
-        new, accum = adagrad_rows(v_table[at, :], as_column(sums[:, at]), grads)
+        new, accum = adagrad_rows(v_table[at, :], v_sums[at, :1], grads)
         v_next[at, :] = new.astype(narrow)
-        sums_next[:, at] = as_line(accum)
+        v_lines[at, :] = jnp.broadcast_to(accum, (TILE, 128))
         go.send(v_next.at[at, :], items_next.at[at, :])
+    for at in tiles(v_items.shape[0]):
+        sums_next[:, at] = jnp.transpose(v_lines[at, :])[:1, :]
     go.finish()
 
 
@@ -227,11 +231,16 @@
     line = pl.BlockSpec(memory_space=pltpu.VMEM)
     return manual(
         functools.partial(peer_body, turn=turn),
-        [pl.BlockSpec(memory_space=pltpu.SMEM), line] + [anywhere()] * 8,
-        [anywhere()] * 3 + [line],
-        [shape(narrow, n, m), shape(narrow, n, d), shape(narrow, m, d), shape(single, 1, m)],
+        [pl.BlockSpec(memory_space=pltpu.SMEM), line, line] + [anywhere()] * 7,
+        [anywhere()] * 4 + [line],
         [
-            pltpu.VMEM((n, d), narrow),
+            shape(narrow, n, d),
+            shape(narrow, n, m),
+            shape(narrow, n, d),
+            shape(narrow, m, d),
+            shape(single, 1, m),
+        ],
+        [
             pltpu.VMEM((d, d), narrow),
             pltpu.VMEM((m, d), narrow),
             pltpu.VMEM((n, m), narrow),
@@ -243,6 +252,8 @@
             pltpu.VMEM((n, m), narrow),
             pltpu.VMEM((n, d), narrow),
             pltpu.VMEM((m, d), narrow),
+            pltpu.VMEM((m, 8), single),
+            pltpu.VMEM((m, 128), single),
         ],
         10 + m // TILE,
         2 * n * d * d + 8 * n * m * d,
@@ -310,15 +321,16 @@
     place, sums, item_sums, table, grad, more, relation, anchor_p, turned_p, items, targets, term,
     users_next, errors, term_keep, term_give, next_a, next_b, sums_next, item_sums_next,
     v_table, v_grad, v_more, v_relation, v_anchor, v_turned, v_items, v_labels, v_term,
-    v_users, v_errors, v_crossed, v_next, sems,
+    v_users, v_errors, v_crossed, v_next, v_sums, v_lines, sems,
     turn,
 ):
     go = Copies(sems)
     n, d = table.shape
     m = items.shape[0]
-    get_more = go.start(more, v_more)
-    get_table = go.start(table, v_table)
-    get_grad = go.start(grad, v_grad)
+    get_table = []
+    for at in tiles(n):
+        for source, target in ((more, v_more), (grad, v_grad), (table, v_table)):
+            get_table.append(go.start(source.at[at, :], target.at[at, :]))
     get_relation = go.start(relation, v_relation)
     get_anchor = go.start(anchor_p, v_anchor.at[n:, :])
     get_items, get_labels = [], []
@@ -331,15 +343,16 @@
             )
     get_turned = go.start(turned_p, v_turned.at[:, n:])
     get_term = go.start(term, v_term)
-    get_more.wait()
-    get_table.wait()
-    get_grad.wait()
-    for at in tiles(n):
+    columns_into(v_sums.at[:n, :], sums[...])
+    columns_into(v_sums.at[n:, :], item_sums[...])
+    for k, at in enumerate(tiles(n)):
+        for copy in get_table[3 * k : 3 * k + 3]:
+            copy.wait()
         new, accum = adagrad_rows(
-            v_table[at, :], as_column(sums[:, at]), v_grad[at, :] + wide(v_more[at, :])
+            v_table[at, :], v_sums[at, :1], wide(v_grad[at, :]) + wide(v_more[at, :])
         )
         v_users[at, :] = new
-        sums_next[:, at] = as_line(accum)
+        v_lines[at, :] = jnp.broadcast_to(accum, (TILE, 128))
         v_turned[:, at] = jnp.transpose(new.astype(narrow))
     go.send(v_users, users_next)
     get_relation.wait()
@@ -364,13 +377,20 @@
     go.send(v_term.at[pl.ds(keep, half), :], term_keep)
     for at in tiles(m):
         grads = dot(v_errors[:, at], v_anchor[...], 0, 0)
-        new, accum = adagrad_rows(wide(v_items[at, :]), as_column(item_sums[:, at]), grads)
+        below = slice(n + at.start, n + at.stop)
+        new, accum = adagrad_rows(wide(v_items[at, :]), v_sums[below, :1], grads)
         v_next[at, :] = new.astype(narrow)
-        item_sums_next[:, at] = as_line(accum)
+        v_lines[below, :] = jnp.broadcast_to(accum, (TILE, 128))
         if at.start < m // 2:
             go.send(v_next.at[at, :], next_a.at[at, :])
         else:
             go.send(v_next.at[at, :], next_b.at[at.start - m // 2 : at.stop - m // 2, :])
+    for at in tiles(n + m):
+        line = jnp.transpose(v_lines[at, :])[:1, :]
+        if at.start < n:
+            sums_next[:, at] = line
+        else:
+            item_sums_next[:, at.start - n : at.stop - n] = line
     go.finish()
 
 
@@ -394,7 +414,7 @@
         ],
         [
             pltpu.VMEM((n, d), single),
-            pltpu.VMEM((n, d), single),
+            pltpu.VMEM((n, d), narrow),
             pltpu.VMEM((n, d), narrow),
             pltpu.VMEM((d, d), narrow),
             pltpu.VMEM((2 * n, d), narrow),
@@ -406,8 +426,10 @@
             pltpu.VMEM((2 * n, m), narrow),
             pltpu.VMEM((d, m), narrow),
             pltpu.VMEM((m, d), narrow),
+            pltpu.VMEM((n + m, 8), single),
+            pltpu.VMEM((n + m, 128), single),
         ],
-        10 + 5 * (m // TILE),
+        8 + 3 * (n // TILE) + 5 * (m // TILE),
         2 * n * d * d + 12 * n * m * d + 2 * m * d * d,
     )(place, sums, item_sums, table, grad, more, relation, anchor_p, turned_p, items, targets, term)
 
@@ -476,7 +498,31 @@
         [shape(single, n, d), shape(single, 1, n)],
         [],
         4 * n * d,
+        limit=16,
     )(table, grad, more, sums)
+
+
+def final_body(place, mine, other, sums, step, sums_next, *, count):
+    half = mine.shape[0]
+    for part, side in ((mine, place[1]), (other, 1 - place[1])):
+        rows = pl.ds(pl.multiple_of(side * half, half), half)
+        grads = wide(part[...]) / count
+        _, accum = adagrad_rows(grads, as_column(sums[:, rows]), grads)
+        step[rows, :] = grads * lax.rsqrt(accum + epsilon)
+        sums_next[:, rows] = as_line(accum)
+
+
+def final(place, mine, other, sums, count):
+    d = mine.shape[1]
+    whole_array = pl.BlockSpec(memory_space=pltpu.VMEM)
+    return pl.pallas_call(
+        functools.partial(final_body, count=count),
+        name="final",
+        in_specs=[pl.BlockSpec(memory_space=pltpu.SMEM)] + [whole_array] * 3,
+        out_specs=[whole_array] * 2,
+        out_shape=[shape(single, d, d), shape(single, 1, d)],
+        compiler_params=pltpu.CompilerParams(vmem_limit_bytes=16 << 20),
+    )(place, mine, other, sums)
 
 
 def pick(parts, key):
@@ -492,7 +538,6 @@
 def relation_total(keep, give):
     blocks = lax.axis_size("blk")
     b, r = lax.axis_index("blk"), lax.axis_index("rel")
-    core = b % 2
     half = keep.shape[0]
     p = keep + exchange(give, 1, 0)
     key = r + 2 * ((b // 2) % 2)
@@ -517,7 +562,7 @@
     sent = parts[0].astype(narrow)
     parts = [sent] + [exchange(sent, 2 * (k // 2), k % 2) for k in (1, 2, 3)]
     p = pick(parts, key)
-    return pick([p, exchange(p, 1, 0)], core)
+    return p, exchange(p, 1, 0)
 
 
 def step(user_table, user_accum, item_table, item_accum, relation, relation_accum, targets):
@@ -529,22 +574,22 @@
 
     mine = user_table.astype(narrow)
     theirs = swap(mine)
-    items, mapped, anchor_o, errors_o, grad_o, grad_ob = first_own(
+    items, mapped, anchor_o, errors_o, grad_ob = first_own(
         place[:1], mine, item_table, relation, targets, 0
     )
     more_p = swap(grad_ob)
     sums_p = swap(sums_o)
-    errors_p, grad_pb, items_next, item_sums = first_peer(
+    users_p, errors_p, grad_pb, items_next, item_sums = first_peer(
         place, theirs, relation, items, targets, mapped, errors_o, anchor_o, item_table, item_sums, 0
     )
     more_o = swap(grad_pb)
     items_next = from_behind(items_next)
     item_sums = from_behind(item_sums)
-    term = first_term(mine, theirs, errors_o, errors_p, items)
-    turned_p, anchor_p = ahead(theirs, grad_pb, more_p, sums_p, relation)
+    term = first_term(mine, users_p, errors_o, errors_p, items)
+    turned_p, anchor_p = ahead(users_p, grad_pb, more_p, sums_p, relation)
 
     users, errors, keep, give, *chunks, sums_o, item_sums = second(
-        place, user_table, grad_o, more_o, sums_o, relation, anchor_p, turned_p,
+        place, user_table, grad_ob, more_o, sums_o, relation, anchor_p, turned_p,
         items_next, item_sums, targets, term, 1,
     )
     grad_o, grad_pb = second_grads(errors, items_next, relation)
@@ -553,12 +598,12 @@
     item_sums = from_behind(item_sums)
     users, sums_o = update_users(users, grad_o, more_o, sums_o)
 
-    total = wide(relation_total(keep, give))
-    mean_grad = total / (blocks * rounds)
-    accum_next = relation_accum + jnp.mean(mean_grad * mean_grad, axis=1)
-    relation_step = mean_grad * lax.rsqrt(accum_next + epsilon)[:, None]
+    relation_step, accum_next = final(
+        place, *relation_total(keep, give), relation_accum[None, :], blocks * rounds
+    )
     items_last = jnp.concatenate([wide(chunk) for chunk in chunks], axis=0)
-    return (users, sums_o[0], items_last, item_sums[0], relation_step, accum_next)
+    item_sums = jnp.maximum(item_sums[0], 0.0)
+    return (users, sums_o[0], items_last, item_sums, relation_step, accum_next[0])
 
 
 def solution(mesh):

time: 128 us -> 118 us (0.922)
  waiting for transfers between devices: 43.5 us -> 38.3 us
  other arithmetic: 10.2 us -> 6.37 us
  starting transfers between devices: 24.7 us -> 22.9 us
    ppermute x16, waiting for transfers between devices: 37.8 us -> 32.7 us  [exchange(): return lax.ppermute(x, ('blk', 'rel'), pairs)]
    pallas_call x0 -> x1, Pallas kernels: none -> 2.15 us  [final(): pl.pallas_call(functools.partial(final_body, count=count), name='final',...]
    ppermute x16, starting transfers between devices: 22.9 us -> 21.1 us  [exchange(): return lax.ppermute(x, ('blk', 'rel'), pairs)]
    mul x2 -> x0, other arithmetic: 1.69 us -> none  [step(): relation_step = mean_grad * lax.rsqrt(accum_next + epsilon)[:, None]]
    pallas_call x1, Pallas kernels: 2.8 us -> 1.5 us  [update_users(): call(users_body, (n // TILE,), [tile, tile, tile, line], [tile, line], [s...]
    unnamed x15 -> x22, local copies, waits for them, and re-layouts: 3.32 us -> 4.41 us
  transfers between devices with their start and end apart: 21 -> 21, of which waited for: 12 -> 10; matrix products, arithmetic and copies ran while one was open for 3% -> 3% of each run, Pallas kernels for 20% -> 20%
where the time goes in v1:
time: 118 us; the launch traced here: 117 us
  Pallas kernels  44.3 us (38%)
  waiting for transfers between devices  38.3 us (32%)
  starting transfers between devices  22.9 us (19%)
  other arithmetic  6.37 us (5%)
  local copies, waits for them, and re-layouts  4.44 us (4%)
    ppermute x16, waiting for transfers between devices, exchange(): return lax.ppermute(x, ('blk', 'rel'), pairs)  32.7 us
    ppermute x16, starting transfers between devices, exchange(): return lax.ppermute(x, ('blk', 'rel'), pairs)  21.1 us
    pallas_call x1, Pallas kernels, second(): manual(functools.partial(second_body, turn=turn), [pl.BlockSpec(memory_sp...  10.7 us
    pallas_call x1, Pallas kernels, first_peer(): manual(functools.partial(peer_body, turn=turn), [pl.BlockSpec(memory_spac...  7.6 us
    pallas_call x1, Pallas kernels, first_own(): call(first_body, (m // TILE,), [whole(n, d), tile, whole(d, d), labels],...  7.54 us
    pallas_call x1, Pallas kernels, first_term(): call(term_body, (m // TILE,), [whole(n, d), whole(n, d), side, side, tile...  6.71 us
    ppermute x5, waiting for transfers between devices, from_behind(): return lax.ppermute(x, 'blk', [(i, (i + 1) % peers) for i in range(peers)])  5.58 us
    pallas_call x1, Pallas kernels, second_grads(): manual(grads_body, [anywhere()] * 3, [anywhere()] * 2, [shape(single, n,...  4.75 us
  transfers between devices with their start and end apart: 21, of which 10 were waited for; matrix products, arithmetic and copies ran while one was open for 3% of the time, Pallas kernels for 20%

profile of v1, /device:TPU:0, one launch (start us, length us, event | category | flops | bytes accessed | tf_op | source)
XLA Modules:
  0.0 117.1 jit_solution(9583636249315548134)
XLA Ops:
  1.9 3.0 %collective-permute-start = (bf16[512,512]{1,0:T(8,128)(2,1)S(1)}, bf16[512,512]{1,0:T(8,128)(2,1)}, u32[]{:S(2)}, u32[]{:S(2)}) collective-permute-start(bf16[512,512]{1,0:T(8,128)(2,1)S(1)} %convert_element_type.41.users.users_o), channel_id=1, source_target_pairs={{0,1},{1,0},{2,3},{3,2},{4,5},{5,4},{6,7},{7,6},{8,9},{9,8},{10,11... | collective-permute-start | bytes 1572872 | tf_op jit(solution)/shard_map/ppermute | solution.py:23
  5.6 7.5 %shard_map.118 = (bf16[1024,512]{1,0:T(8,128)(2,1)}, bf16[1024,512]{1,0:T(8,128)(2,1)}, bf16[512,512]{1,0:T(8,128)(2,1)}, bf16[512,1024]{1,0:T(8,128)(2,1)}, bf16[512,512]{1,0:T(8,128)(2,1)}) custom-call(s32[1]{0:T(128)} %bitcast.place, bf16[512,512]{1,0:T(8,128)(2,1)} %copy-done.5, f32[1024,512]{1,0:T(8,128)} %table.2, bf16[512,512]{1,0:T(8,128)(2,1)} %relation.9, ...), custom_call_target="tpu_custom_call" | custom-call | flops 1879048192 | bytes 4194304 | tf_op jit(solution)/shard_map/pallas_call | solution.py:160
  13.1 3.9 %collective-permute-done.users = bf16[512,512]{1,0:T(8,128)(2,1)} collective-permute-done((bf16[512,512]{1,0:T(8,128)(2,1)S(1)}, bf16[512,512]{1,0:T(8,128)(2,1)}, u32[]{:S(2)}, u32[]{:S(2)}) %collective-permute-start) | collective-permute-done | bytes 524320 | tf_op jit(solution)/shard_map/ppermute | solution.py:23
  17.0 7.6 %shard_map.119 = (bf16[512,512]{1,0:T(8,128)(2,1)}, bf16[512,1024]{1,0:T(8,128)(2,1)}, bf16[512,512]{1,0:T(8,128)(2,1)}, bf16[1024,512]{1,0:T(8,128)(2,1)}, f32[1,1024]{1,0:T(1,128)}) custom-call(s32[2]{0:T(128)} %pad_add_fusion.place, f32[1,1024]{1,0:T(1,128)} %bitcast.9, bf16[512,512]{1,0:T(8,128)(2,1)} %collective-permute-done.users, ...), custom_call_target="tpu_custom_call" | custom-call | flops 2415919104 | bytes 4194304 | tf_op jit(solution)/shard_map/pallas_call | solution.py:232
  24.7 1.8 %collective-permute-start.3 = (bf16[512,512]{1,0:T(8,128)(2,1)}, bf16[512,512]{1,0:T(8,128)(2,1)S(1)}, u32[]{:S(2)}, u32[]{:S(2)}) collective-permute-start(bf16[512,512]{1,0:T(8,128)(2,1)} %get-tuple-element.37.grad), channel_id=1, source_target_pairs={{0,1},{1,0},{2,3},{3,2},{4,5},{5,4},{6,7},{7,6},{8,9},{9,8},{10,11... | collective-permute-start | bytes 1572872 | tf_op jit(solution)/shard_map/ppermute | solution.py:23
  26.8 1.7 %collective-permute-start.4 = (f32[1,512]{1,0:T(1,128)S(1)}, f32[1,512]{1,0:T(1,128)S(1)}, u32[]{:S(2)}, u32[]{:S(2)}) collective-permute-start(f32[1,512]{1,0:T(1,128)S(1)} %bitcast.12), channel_id=1, source_target_pairs={{0,1},{1,0},{2,3},{3,2},{4,5},{5,4},{6,7},{7,6},{8,9},{9,8},{10,11... | collective-permute-start | bytes 6152 | tf_op jit(solution)/shard_map/ppermute | solution.py:23
  29.2 6.7 %shard_map.121.term = f32[512,512]{1,0:T(8,128)} custom-call(bf16[512,512]{1,0:T(8,128)(2,1)} %copy-done.5, bf16[512,512]{1,0:T(8,128)(2,1)} %get-tuple-element.39.table.users_p, bf16[512,1024]{1,0:T(8,128)(2,1)} %get-tuple-element.34.errors_o, bf16[512,1024]{1,0:T(8,128)(2,1)} %get-tuple-element.43.errors_p, bf16[1024,512]{1,0:T(8,128)(2,1)} %get-tuple-element.32.items_b.items), custom_call_target="tpu_custom_call" | custom-call | flops 1610612736 | bytes 4194304 | tf_op jit(solution)/shard_map/pallas_call | solution.py:309
  35.9 14.3 %collective-permute-done.4.sums = f32[1,512]{1,0:T(1,128)S(1)} collective-permute-done((f32[1,512]{1,0:T(1,128)S(1)}, f32[1,512]{1,0:T(1,128)S(1)}, u32[]{:S(2)}, u32[]{:S(2)}) %collective-permute-start.4) | collective-permute-done | bytes 2080 | tf_op jit(solution)/shard_map/ppermute | solution.py:23
  51.6 3.4 %shard_map.120 = (bf16[512,512]{1,0:T(8,128)(2,1)}, bf16[512,512]{1,0:T(8,128)(2,1)}) custom-call(bf16[512,512]{1,0:T(8,128)(2,1)} %get-tuple-element.39.table.users_p, bf16[512,512]{1,0:T(8,128)(2,1)} %get-tuple-element.38.grad, bf16[512,512]{1,0:T(8,128)(2,1)} %copy-done.6, f32[1,512]{1,0:T(1,128)} %copy-done.7, bf16[512,512]{1,0:T(8,128)(2,1)} %relation.9), custom_call_target="tpu_custom_call" | custom-call | flops 268435456 | bytes 4194304 | tf_op jit(solution)/shard_map/pallas_call | solution.py:273
  55.6 10.7 %shard_map.122 = (f32[512,512]{1,0:T(8,128)}, bf16[1024,1024]{1,0:T(8,128)(2,1)}, f32[256,512]{1,0:T(8,128)}, f32[256,512]{1,0:T(8,128)}, bf16[512,512]{1,0:T(8,...) custom-call(s32[2]{0:T(128)} %pad_add_fusion.place, f32[1,512]{1,0:T(1,128)} %bitcast.11, ...), custom_call_target="tpu_custom_call" | custom-call | flops 4026531840 | bytes 4194304 | tf_op jit(solution)/shard_map/pallas_call | solution.py:401
  67.0 1.7 %collective-permute-done.10 = f32[256,512]{1,0:T(8,128)S(1)} collective-permute-done((f32[256,512]{1,0:T(8,128)}, f32[256,512]{1,0:T(8,128)S(1)}, u32[]{:S(2)}, u32[]{:S(2)}) %collective-permute-start.10) | collective-permute-done | bytes 524320 | tf_op jit(solution)/shard_map/ppermute | solution.py:23
  70.0 2.8 %collective-permute-start.11 = (bf16[64,512]{1,0:T(8,128)(2,1)S(1)}, bf16[64,512]{1,0:T(8,128)(2,1)S(1)}, u32[]{:S(2)}, u32[]{:S(2)}) collective-permute-start(bf16[64,512]{1,0:T(8,128)(2,1)S(1)} %get-tuple-element.58), channel_id=1, source_target_pairs={{0,5},{1,4},{2,7},{3,6},{4,1},{5,0},{6,3},{7,2},{8,13},{9,12},{10,... | collective-permute-start | bytes 196616 | tf_op jit(solution)/shard_map/ppermute | solution.py:23
  73.5 1.8 %collective-permute-done.11 = bf16[64,512]{1,0:T(8,128)(2,1)S(1)} collective-permute-done((bf16[64,512]{1,0:T(8,128)(2,1)S(1)}, bf16[64,512]{1,0:T(8,128)(2,1)S(1)}, u32[]{:S(2)}, u32[]{:S(2)}) %collective-permute-start.11) | collective-permute-done | bytes 65568 | tf_op jit(solution)/shard_map/ppermute | solution.py:23
  75.4 1.7 %collective-permute-done.12 = bf16[64,512]{1,0:T(8,128)(2,1)S(1)} collective-permute-done((bf16[64,512]{1,0:T(8,128)(2,1)S(1)}, bf16[64,512]{1,0:T(8,128)(2,1)S(1)}, u32[]{:S(2)}, u32[]{:S(2)}) %collective-permute-start.12) | collective-permute-done | bytes 65568 | tf_op jit(solution)/shard_map/ppermute | solution.py:23
  77.6 1.6 %collective-permute-start.14 = (bf16[64,512]{1,0:T(8,128)(2,1)S(1)}, bf16[64,512]{1,0:T(8,128)(2,1)S(1)}, u32[]{:S(2)}, u32[]{:S(2)}) collective-permute-start(bf16[64,512]{1,0:T(8,128)(2,1)S(1)} %add_convert_fusion.1), channel_id=1, source_target_pairs={{0,8},{1,9},{2,10},{3,11},{4,12},{5,13},{6,14},{7,15},{8,0},{9,1},... | collective-permute-start | bytes 196616 | tf_op jit(solution)/shard_map/ppermute | solution.py:23
  79.2 2.1 %collective-permute-start.15 = (bf16[64,512]{1,0:T(8,128)(2,1)S(1)}, bf16[64,512]{1,0:T(8,128)(2,1)S(1)}, u32[]{:S(2)}, u32[]{:S(2)}) collective-permute-start(bf16[64,512]{1,0:T(8,128)(2,1)S(1)} %add_convert_fusion.1), channel_id=1, source_target_pairs={{0,16},{1,17},{2,18},{3,19},{4,20},{5,21},{6,22},{7,23},{8,24},{9,... | collective-permute-start | bytes 196616 | tf_op jit(solution)/shard_map/ppermute | solution.py:23
  83.1 2.7 %collective-permute-done.15 = bf16[64,512]{1,0:T(8,128)(2,1)S(1)} collective-permute-done((bf16[64,512]{1,0:T(8,128)(2,1)S(1)}, bf16[64,512]{1,0:T(8,128)(2,1)S(1)}, u32[]{:S(2)}, u32[]{:S(2)}) %collective-permute-start.15) | collective-permute-done | bytes 65568 | tf_op jit(solution)/shard_map/ppermute | solution.py:23
  87.4 2.3 %collective-permute-start.17 = (bf16[64,512]{1,0:T(8,128)(2,1)S(1)}, bf16[64,512]{1,0:T(8,128)(2,1)S(1)}, u32[]{:S(2)}, u32[]{:S(2)}) collective-permute-start(bf16[64,512]{1,0:T(8,128)(2,1)S(1)} %add_convert_fusion), channel_id=1, source_target_pairs={{0,5},{1,4},{2,7},{3,6},{4,1},{5,0},{6,3},{7,2},{8,13},{9,12},{10,... | collective-permute-start | bytes 196616 | tf_op jit(solution)/shard_map/ppermute | solution.py:23
  91.0 4.7 %shard_map.123 = (f32[512,512]{1,0:T(8,128)}, bf16[512,512]{1,0:T(8,128)(2,1)}) custom-call(bf16[1024,1024]{1,0:T(8,128)(2,1)} %get-tuple-element.45.errors, bf16[1024,512]{1,0:T(8,128)(2,1)} %collective-permute-done.5.items, bf16[512,512]{1,0:T(8,128)(2,1)} %relation.9), custom_call_target="tpu_custom_call" | custom-call | flops 1610612736 | bytes 4194304 | tf_op jit(solution)/shard_map/pallas_call | solution.py:465
  95.8 1.8 %collective-permute-start.6 = (bf16[512,512]{1,0:T(8,128)(2,1)}, bf16[512,512]{1,0:T(8,128)(2,1)S(1)}, u32[]{:S(2)}, u32[]{:S(2)}) collective-permute-start(bf16[512,512]{1,0:T(8,128)(2,1)} %get-tuple-element.47), channel_id=1, source_target_pairs={{0,1},{1,0},{2,3},{3,2},{4,5},{5,4},{6,7},{7,6},{8,9},{9,8},{10,11... | collective-permute-start | bytes 1572872 | tf_op jit(solution)/shard_map/ppermute | solution.py:23
  97.6 4.4 %collective-permute-done.18 = bf16[64,512]{1,0:T(8,128)(2,1)S(1)} collective-permute-done((bf16[64,512]{1,0:T(8,128)(2,1)S(1)}, bf16[64,512]{1,0:T(8,128)(2,1)S(1)}, u32[]{:S(2)}, u32[]{:S(2)}) %collective-permute-start.18) | collective-permute-done | bytes 65568 | tf_op jit(solution)/shard_map/ppermute | solution.py:23
  102.1 5.6 %collective-permute-done.9 = f32[1,1024]{1,0:T(1,128)S(1)} collective-permute-done((f32[1,1024]{1,0:T(1,128)S(1)}, f32[1,1024]{1,0:T(1,128)S(1)}, u32[]{:S(2)}, u32[]{:S(2)}) %collective-permute-start.9) | collective-permute-done | bytes 4128 | tf_op jit(solution)/shard_map/ppermute | solution.py:32
  112.3 2.7 %maximum_convert_fusion = f32[1024,512]{1,0:T(8,128)} fusion(bf16[512,512]{1,0:T(8,128)(2,1)} %collective-permute-done.8, bf16[512,512]{1,0:T(8,128)(2,1)S(1)} %collective-permute-done.7), kind=kLoop, calls=%fused_computation | loop fusion | flops 2097152 | bytes 3145728 | tf_op jit(solution)/shard_map/concatenate | solution.py:604
  114.9 2.1 %final.1 = (f32[512,512]{1,0:T(8,128)}, f32[1,512]{1,0:T(1,128)}) custom-call(s32[2]{0:T(128)S(1)} %copy-done.3, bf16[256,512]{1,0:T(8,128)(2,1)S(1)} %pad_maximum_fusion.mine, bf16[256,512]{1,0:T(8,128)(2,1)S(1)} %collective-permute-done.20.other, f32[1,512]{1,0:T(1,128)S(1)} %bitcast.8), custom_call_target="tpu_custom_call" | custom-call | tf_op jit(solution)/shard_map/final/pallas_call | solution.py:518
  (58 shorter events, 17.5 us)
Async XLA Ops:
  1.9 15.1 %collective-permute-start = (bf16[512,512]{1,0:T(8,128)(2,1)S(1)}, bf16[512,512]{1,0:T(8,128)(2,1)}, u32[]{:S(2)}, u32[]{:S(2)}) collective-permute-start(bf16[512,512]{1,0:T(8,128)(2,1)S(1)} %convert_element_type.41.users.users_o), channel_id=1, source_target_pairs={{0,1},{1,0},{2,3},{3,2},{4,5},{5,4},{6,7},{7,6},{8,9},{9,8},{10,11... | collective-permute-start | bytes 1572872 | tf_op jit(solution)/shard_map/ppermute | solution.py:23
  17.0 9.8 %copy-start.10 = (f32[512]{0:T(512)S(1)}, f32[512]{0:T(512)}, u32[]{:S(2)}) copy-start(f32[512]{0:T(512)} %param.8) | copy-start | bytes 6148
  24.6 30.4 %collective-permute-start.5 = (bf16[1024,512]{1,0:T(8,128)(2,1)}, bf16[1024,512]{1,0:T(8,128)(2,1)}, u32[]{:S(2)}, u32[]{:S(2)}) collective-permute-start(bf16[1024,512]{1,0:T(8,128)(2,1)} %get-tuple-element.42), channel_id=1, source_target_pairs={{0,2},{2,4},{4,6},{6,8},{8,10},{10,12},{12,14},{14,16},{16,18},{18... | collective-permute-start | bytes 3145736 | tf_op jit(solution)/shard_map/ppermute | solution.py:32
  24.7 25.6 %collective-permute-start.3 = (bf16[512,512]{1,0:T(8,128)(2,1)}, bf16[512,512]{1,0:T(8,128)(2,1)S(1)}, u32[]{:S(2)}, u32[]{:S(2)}) collective-permute-start(bf16[512,512]{1,0:T(8,128)(2,1)} %get-tuple-element.37.grad), channel_id=1, source_target_pairs={{0,1},{1,0},{2,3},{3,2},{4,5},{5,4},{6,7},{7,6},{8,9},{9,8},{10,11... | collective-permute-start | bytes 1572872 | tf_op jit(solution)/shard_map/ppermute | solution.py:23
  26.5 28.5 %collective-permute-start.2 = (bf16[512,512]{1,0:T(8,128)(2,1)}, bf16[512,512]{1,0:T(8,128)(2,1)}, u32[]{:S(2)}, u32[]{:S(2)}) collective-permute-start(bf16[512,512]{1,0:T(8,128)(2,1)} %get-tuple-element.38.grad), channel_id=1, source_target_pairs={{0,1},{1,0},{2,3},{3,2},{4,5},{5,4},{6,7},{7,6},{8,9},{9,8},{10,11... | collective-permute-start | bytes 1572872 | tf_op jit(solution)/shard_map/ppermute | solution.py:23
  26.8 23.5 %collective-permute-start.4 = (f32[1,512]{1,0:T(1,128)S(1)}, f32[1,512]{1,0:T(1,128)S(1)}, u32[]{:S(2)}, u32[]{:S(2)}) collective-permute-start(f32[1,512]{1,0:T(1,128)S(1)} %bitcast.12), channel_id=1, source_target_pairs={{0,1},{1,0},{2,3},{3,2},{4,5},{5,4},{6,7},{7,6},{8,9},{9,8},{10,11... | collective-permute-start | bytes 6152 | tf_op jit(solution)/shard_map/ppermute | solution.py:23
  28.5 26.5 %collective-permute-start.1 = (f32[1,1024]{1,0:T(1,128)}, f32[1,1024]{1,0:T(1,128)S(1)}, u32[]{:S(2)}, u32[]{:S(2)}) collective-permute-start(f32[1,1024]{1,0:T(1,128)} %get-tuple-element.36), channel_id=1, source_target_pairs={{0,2},{2,4},{4,6},{6,8},{8,10},{10,12},{12,14},{14,16},{16,18},{18... | collective-permute-start | bytes 12296 | tf_op jit(solution)/shard_map/ppermute | solution.py:32
  66.3 2.5 %collective-permute-start.10 = (f32[256,512]{1,0:T(8,128)}, f32[256,512]{1,0:T(8,128)S(1)}, u32[]{:S(2)}, u32[]{:S(2)}) collective-permute-start(f32[256,512]{1,0:T(8,128)} %get-tuple-element.55), channel_id=1, source_target_pairs={{0,2},{1,3},{2,0},{3,1},{4,6},{5,7},{6,4},{7,5},{8,10},{9,11},{10,... | collective-permute-start | bytes 1572872 | tf_op jit(solution)/shard_map/ppermute | solution.py:23
  70.0 5.4 %collective-permute-start.11 = (bf16[64,512]{1,0:T(8,128)(2,1)S(1)}, bf16[64,512]{1,0:T(8,128)(2,1)S(1)}, u32[]{:S(2)}, u32[]{:S(2)}) collective-permute-start(bf16[64,512]{1,0:T(8,128)(2,1)S(1)} %get-tuple-element.58), channel_id=1, source_target_pairs={{0,5},{1,4},{2,7},{3,6},{4,1},{5,0},{6,3},{7,2},{8,13},{9,12},{10,... | collective-permute-start | bytes 196616 | tf_op jit(solution)/shard_map/ppermute | solution.py:23
  72.7 4.3 %collective-permute-start.12 = (bf16[64,512]{1,0:T(8,128)(2,1)S(1)}, bf16[64,512]{1,0:T(8,128)(2,1)S(1)}, u32[]{:S(2)}, u32[]{:S(2)}) collective-permute-start(bf16[64,512]{1,0:T(8,128)(2,1)S(1)} %get-tuple-element.60), channel_id=1, source_target_pairs={{0,1},{1,0},{2,3},{3,2},{4,5},{5,4},{6,7},{7,6},{8,9},{9,8},{10,11... | collective-permute-start | bytes 196616 | tf_op jit(solution)/shard_map/ppermute | solution.py:23
  73.3 4.3 %collective-permute-start.13 = (bf16[64,512]{1,0:T(8,128)(2,1)S(1)}, bf16[64,512]{1,0:T(8,128)(2,1)S(1)}, u32[]{:S(2)}, u32[]{:S(2)}) collective-permute-start(bf16[64,512]{1,0:T(8,128)(2,1)S(1)} %get-tuple-element.59), channel_id=1, source_target_pairs={{0,4},{1,5},{2,6},{3,7},{4,0},{5,1},{6,2},{7,3},{8,12},{9,13},{10,... | collective-permute-start | bytes 196616 | tf_op jit(solution)/shard_map/ppermute | solution.py:23
  77.6 5.5 %collective-permute-start.14 = (bf16[64,512]{1,0:T(8,128)(2,1)S(1)}, bf16[64,512]{1,0:T(8,128)(2,1)S(1)}, u32[]{:S(2)}, u32[]{:S(2)}) collective-permute-start(bf16[64,512]{1,0:T(8,128)(2,1)S(1)} %add_convert_fusion.1), channel_id=1, source_target_pairs={{0,8},{1,9},{2,10},{3,11},{4,12},{5,13},{6,14},{7,15},{8,0},{9,1},... | collective-permute-start | bytes 196616 | tf_op jit(solution)/shard_map/ppermute | solution.py:23
  79.2 6.6 %collective-permute-start.15 = (bf16[64,512]{1,0:T(8,128)(2,1)S(1)}, bf16[64,512]{1,0:T(8,128)(2,1)S(1)}, u32[]{:S(2)}, u32[]{:S(2)}) collective-permute-start(bf16[64,512]{1,0:T(8,128)(2,1)S(1)} %add_convert_fusion.1), channel_id=1, source_target_pairs={{0,16},{1,17},{2,18},{3,19},{4,20},{5,21},{6,22},{7,23},{8,24},{9,... | collective-permute-start | bytes 196616 | tf_op jit(solution)/shard_map/ppermute | solution.py:23
  81.3 6.1 %collective-permute-start.16 = (bf16[64,512]{1,0:T(8,128)(2,1)S(1)}, bf16[64,512]{1,0:T(8,128)(2,1)S(1)}, u32[]{:S(2)}, u32[]{:S(2)}) collective-permute-start(bf16[64,512]{1,0:T(8,128)(2,1)S(1)} %add_convert_fusion.1), channel_id=1, source_target_pairs={{0,24},{1,25},{2,26},{3,27},{4,28},{5,29},{6,30},{7,31},{8,16},{9,... | collective-permute-start | bytes 196616 | tf_op jit(solution)/shard_map/ppermute | solution.py:23
  82.0 30.2 %collective-permute-start.7 = (bf16[512,512]{1,0:T(8,128)(2,1)}, bf16[512,512]{1,0:T(8,128)(2,1)S(1)}, u32[]{:S(2)}, u32[]{:S(2)}) collective-permute-start(bf16[512,512]{1,0:T(8,128)(2,1)} %get-tuple-element.51), channel_id=1, source_target_pairs={{0,2},{2,4},{4,6},{6,8},{8,10},{10,12},{12,14},{14,16},{16,18},{18... | collective-permute-start | bytes 1572872 | tf_op jit(solution)/shard_map/ppermute | solution.py:32
  82.0 30.2 %collective-permute-start.8 = (bf16[512,512]{1,0:T(8,128)(2,1)}, bf16[512,512]{1,0:T(8,128)(2,1)}, u32[]{:S(2)}, u32[]{:S(2)}) collective-permute-start(bf16[512,512]{1,0:T(8,128)(2,1)} %get-tuple-element.52), channel_id=1, source_target_pairs={{0,2},{2,4},{4,6},{6,8},{8,10},{10,12},{12,14},{14,16},{16,18},{18... | collective-permute-start | bytes 1572872 | tf_op jit(solution)/shard_map/ppermute | solution.py:32
  87.4 8.3 %collective-permute-start.17 = (bf16[64,512]{1,0:T(8,128)(2,1)S(1)}, bf16[64,512]{1,0:T(8,128)(2,1)S(1)}, u32[]{:S(2)}, u32[]{:S(2)}) collective-permute-start(bf16[64,512]{1,0:T(8,128)(2,1)S(1)} %add_convert_fusion), channel_id=1, source_target_pairs={{0,5},{1,4},{2,7},{3,6},{4,1},{5,0},{6,3},{7,2},{8,13},{9,12},{10,... | collective-permute-start | bytes 196616 | tf_op jit(solution)/shard_map/ppermute | solution.py:23
  89.7 12.2 %collective-permute-start.18 = (bf16[64,512]{1,0:T(8,128)(2,1)S(1)}, bf16[64,512]{1,0:T(8,128)(2,1)S(1)}, u32[]{:S(2)}, u32[]{:S(2)}) collective-permute-start(bf16[64,512]{1,0:T(8,128)(2,1)S(1)} %add_convert_fusion), channel_id=1, source_target_pairs={{0,4},{1,5},{2,6},{3,7},{4,0},{5,1},{6,2},{7,3},{8,12},{9,13},{10,... | collective-permute-start | bytes 196616 | tf_op jit(solution)/shard_map/ppermute | solution.py:23
  90.7 11.3 %collective-permute-start.19 = (bf16[64,512]{1,0:T(8,128)(2,1)S(1)}, bf16[64,512]{1,0:T(8,128)(2,1)S(1)}, u32[]{:S(2)}, u32[]{:S(2)}) collective-permute-start(bf16[64,512]{1,0:T(8,128)(2,1)S(1)} %add_convert_fusion), channel_id=1, source_target_pairs={{0,1},{1,0},{2,3},{3,2},{4,5},{5,4},{6,7},{7,6},{8,9},{9,8},{10,11... | collective-permute-start | bytes 196616 | tf_op jit(solution)/shard_map/ppermute | solution.py:23
  91.0 11.0 %copy-start.8 = (f32[1,1024]{1,0:T(1,128)S(1)}, f32[1,1024]{1,0:T(1,128)}, u32[]{:S(2)}) copy-start(f32[1,1024]{1,0:T(1,128)} %get-tuple-element.53) | copy-start | bytes 12292
  91.0 17.3 %copy-start.4 = (f32[1,512]{1,0:T(1,128)S(1)}, f32[1,512]{1,0:T(1,128)}, u32[]{:S(2)}) copy-start(f32[1,512]{1,0:T(1,128)} %get-tuple-element.48.sums) | copy-start | bytes 6148
  95.8 12.5 %collective-permute-start.6 = (bf16[512,512]{1,0:T(8,128)(2,1)}, bf16[512,512]{1,0:T(8,128)(2,1)S(1)}, u32[]{:S(2)}, u32[]{:S(2)}) collective-permute-start(bf16[512,512]{1,0:T(8,128)(2,1)} %get-tuple-element.47), channel_id=1, source_target_pairs={{0,1},{1,0},{2,3},{3,2},{4,5},{5,4},{6,7},{7,6},{8,9},{9,8},{10,11... | collective-permute-start | bytes 1572872 | tf_op jit(solution)/shard_map/ppermute | solution.py:23
  102.0 5.7 %collective-permute-start.9 = (f32[1,1024]{1,0:T(1,128)S(1)}, f32[1,1024]{1,0:T(1,128)S(1)}, u32[]{:S(2)}, u32[]{:S(2)}) collective-permute-start(f32[1,1024]{1,0:T(1,128)S(1)} %copy-done.8), channel_id=1, source_target_pairs={{0,2},{2,4},{4,6},{6,8},{8,10},{10,12},{12,14},{14,16},{16,18},{18... | collective-permute-start | bytes 12296 | tf_op jit(solution)/shard_map/ppermute | solution.py:32
  102.0 12.9 %collective-permute-start.20 = (bf16[256,512]{1,0:T(8,128)(2,1)S(1)}, bf16[256,512]{1,0:T(8,128)(2,1)S(1)}, u32[]{:S(2)}, u32[]{:S(2)}) collective-permute-start(bf16[256,512]{1,0:T(8,128)(2,1)S(1)} %pad_maximum_fusion.mine), channel_id=1, source_target_pairs={{0,2},{1,3},{2,0},{3,1},{4,6},{5,7},{6,4},{7,5},{8,10},{9,11},{10,... | collective-permute-start | bytes 786440 | tf_op jit(solution)/shard_map/ppermute | solution.py:23
  (8 other events, 13.4 us)

commit v2 on v1

--- a/solution.py
+++ b/solution.py
@@ -190,23 +190,25 @@
 ):
     go = Copies(sems)
     n = users.shape[0]
-    peer_rows = pl.ds(pl.multiple_of((1 - place[0]) * n, n), n)
     get_relation = go.start(relation, v_relation)
-    go.send(users, users_b)
     get_items = go.start(items_b, v_items)
-    get_labels = go.start(targets.at[turn, peer_rows], v_labels)
+    get_labels = []
+    for at in tiles(n):
+        rows = pl.ds(pl.multiple_of((1 - place[0]) * n + at.start, TILE), TILE)
+        get_labels.append(go.start(targets.at[turn, rows], v_labels.at[at, :]))
     get_mapped = go.start(mapped, v_mapped)
     get_errors = go.start(errors_o, v_errors_o)
     get_anchor = go.start(anchor_o, v_anchor_o)
     get_table = go.start(table, v_table)
+    go.send(users, users_b)
     columns_into(v_sums, sums[...])
     get_relation.wait()
     v_anchor[...] = dot(users[...], v_relation[...], 1, 0).astype(narrow)
     get_items.wait()
-    get_labels.wait()
-    for at in tiles(v_items.shape[0]):
-        scores = dot(v_anchor[...], v_items[at, :], 1, 1)
-        v_errors[:, at] = errors_of(scores, v_labels[:, at])
+    for at, copy in zip(tiles(n), get_labels):
+        copy.wait()
+        scores = dot(v_anchor[at, :], v_items[...], 1, 1)
+        v_errors[at, :] = errors_of(scores, v_labels[at, :])
     go.send(v_errors, errors_p)
     get_mapped.wait()
     v_grad[...] = dot(v_errors[...], v_mapped[...], 1, 0).astype(narrow)
@@ -255,7 +257,7 @@
             pltpu.VMEM((m, 8), single),
             pltpu.VMEM((m, 128), single),
         ],
-        10 + m // TILE,
+        10 + n // TILE + m // TILE,
         2 * n * d * d + 8 * n * m * d,
     )(place, sums, users, relation, items_b, targets, mapped, errors_o, anchor_o, table)
 
@@ -333,13 +335,13 @@
             get_table.append(go.start(source.at[at, :], target.at[at, :]))
     get_relation = go.start(relation, v_relation)
     get_anchor = go.start(anchor_p, v_anchor.at[n:, :])
-    get_items, get_labels = [], []
-    for at in tiles(m):
-        get_items.append(go.start(items.at[at, :], v_items.at[at, :]))
-        for half, first in ((0, place[0]), (1, 1 - place[0])):
-            rows = pl.ds(pl.multiple_of(first * n, n), n)
+    get_items = go.start(items, v_items)
+    get_labels = []
+    for half, first in ((0, place[0]), (n, 1 - place[0])):
+        for at in tiles(n):
+            rows = pl.ds(pl.multiple_of(first * n + at.start, TILE), TILE)
             get_labels.append(
-                go.start(targets.at[turn, rows, at], v_labels.at[half * n : half * n + n, at])
+                go.start(targets.at[turn, rows], v_labels.at[half + at.start : half + at.stop, :])
             )
     get_turned = go.start(turned_p, v_turned.at[:, n:])
     get_term = go.start(term, v_term)
@@ -357,14 +359,14 @@
     go.send(v_users, users_next)
     get_relation.wait()
     v_anchor[:n, :] = dot(v_users[...].astype(narrow), v_relation[...], 1, 0).astype(narrow)
-    get_anchor.wait()
-    for k, at in enumerate(tiles(m)):
-        get_items[k].wait()
-        get_labels[2 * k].wait()
-        get_labels[2 * k + 1].wait()
-        scores = dot(v_anchor[...], v_items[at, :], 1, 1)
-        v_errors[:, at] = errors_of(scores, v_labels[:, at])
-        go.send(v_errors.at[:, at], errors.at[:, at])
+    get_items.wait()
+    for at, copy in zip(tiles(2 * n), get_labels):
+        if at.start == n:
+            get_anchor.wait()
+        copy.wait()
+        scores = dot(v_anchor[at, :], v_items[...], 1, 1)
+        v_errors[at, :] = errors_of(scores, v_labels[at, :])
+        go.send(v_errors.at[at, :], errors.at[at, :])
     get_turned.wait()
     get_term.wait()
     for at in tiles(d):
@@ -429,7 +431,7 @@
             pltpu.VMEM((n + m, 8), single),
             pltpu.VMEM((n + m, 128), single),
         ],
-        8 + 3 * (n // TILE) + 5 * (m // TILE),
+        9 + 7 * (n // TILE) + m // TILE,
         2 * n * d * d + 12 * n * m * d + 2 * m * d * d,
     )(place, sums, item_sums, table, grad, more, relation, anchor_p, turned_p, items, targets, term)
 

time: 118 us -> 117 us (level)
  transfers between devices with their start and end apart: 21 -> 21, of which waited for: 10 -> 10; matrix products, arithmetic and copies ran while one was open for 3% -> 3% of each run, Pallas kernels for 20% -> 21%
where the time goes in v2:
time: 117 us; the launch traced here: 116 us
  Pallas kernels  43.3 us (37%)
  waiting for transfers between devices  38.3 us (33%)
  starting transfers between devices  22.9 us (20%)
  other arithmetic  6.37 us (5%)
  local copies, waits for them, and re-layouts  4.44 us (4%)
    ppermute x16, waiting for transfers between devices, exchange(): return lax.ppermute(x, ('blk', 'rel'), pairs)  32.7 us
    ppermute x16, starting transfers between devices, exchange(): return lax.ppermute(x, ('blk', 'rel'), pairs)  21.1 us
    pallas_call x1, Pallas kernels, second(): manual(functools.partial(second_body, turn=turn), [pl.BlockSpec(memory_sp...  9.61 us
    pallas_call x1, Pallas kernels, first_peer(): manual(functools.partial(peer_body, turn=turn), [pl.BlockSpec(memory_spac...  7.67 us
    pallas_call x1, Pallas kernels, first_own(): call(first_body, (m // TILE,), [whole(n, d), tile, whole(d, d), labels],...  7.54 us
    pallas_call x1, Pallas kernels, first_term(): call(term_body, (m // TILE,), [whole(n, d), whole(n, d), side, side, tile...  6.71 us
    ppermute x5, waiting for transfers between devices, from_behind(): return lax.ppermute(x, 'blk', [(i, (i + 1) % peers) for i in range(peers)])  5.58 us
    pallas_call x1, Pallas kernels, second_grads(): manual(grads_body, [anywhere()] * 3, [anywhere()] * 2, [shape(single, n,...  4.74 us
  transfers between devices with their start and end apart: 21, of which 10 were waited for; matrix products, arithmetic and copies ran while one was open for 3% of the time, Pallas kernels for 21%

profile of v2, /device:TPU:0, one launch (start us, length us, event | category | flops | bytes accessed | tf_op | source)
XLA Modules:
  0.0 116.1 jit_solution(11966908393971172700)
XLA Ops:
  1.9 3.0 %collective-permute-start = (bf16[512,512]{1,0:T(8,128)(2,1)S(1)}, bf16[512,512]{1,0:T(8,128)(2,1)}, u32[]{:S(2)}, u32[]{:S(2)}) collective-permute-start(bf16[512,512]{1,0:T(8,128)(2,1)S(1)} %convert_element_type.41.users.users_o), channel_id=1, source_target_pairs={{0,1},{1,0},{2,3},{3,2},{4,5},{5,4},{6,7},{7,6},{8,9},{9,8},{10,11... | collective-permute-start | bytes 1572872 | tf_op jit(solution)/shard_map/ppermute | solution.py:23
  5.6 7.5 %shard_map.118 = (bf16[1024,512]{1,0:T(8,128)(2,1)}, bf16[1024,512]{1,0:T(8,128)(2,1)}, bf16[512,512]{1,0:T(8,128)(2,1)}, bf16[512,1024]{1,0:T(8,128)(2,1)}, bf16[512,512]{1,0:T(8,128)(2,1)}) custom-call(s32[1]{0:T(128)} %bitcast.place, bf16[512,512]{1,0:T(8,128)(2,1)} %copy-done.5, f32[1024,512]{1,0:T(8,128)} %table.2, bf16[512,512]{1,0:T(8,128)(2,1)} %relation.9, ...), custom_call_target="tpu_custom_call" | custom-call | flops 1879048192 | bytes 4194304 | tf_op jit(solution)/shard_map/pallas_call | solution.py:160
  13.1 3.9 %collective-permute-done.users = bf16[512,512]{1,0:T(8,128)(2,1)} collective-permute-done((bf16[512,512]{1,0:T(8,128)(2,1)S(1)}, bf16[512,512]{1,0:T(8,128)(2,1)}, u32[]{:S(2)}, u32[]{:S(2)}) %collective-permute-start) | collective-permute-done | bytes 524320 | tf_op jit(solution)/shard_map/ppermute | solution.py:23
  17.0 7.7 %shard_map.119 = (bf16[512,512]{1,0:T(8,128)(2,1)}, bf16[512,1024]{1,0:T(8,128)(2,1)}, bf16[512,512]{1,0:T(8,128)(2,1)}, bf16[1024,512]{1,0:T(8,128)(2,1)}, f32[1,1024]{1,0:T(1,128)}) custom-call(s32[2]{0:T(128)} %pad_add_fusion.place, f32[1,1024]{1,0:T(1,128)} %bitcast.9, bf16[512,512]{1,0:T(8,128)(2,1)} %collective-permute-done.users, ...), custom_call_target="tpu_custom_call" | custom-call | flops 2415919104 | bytes 4194304 | tf_op jit(solution)/shard_map/pallas_call | solution.py:234
  24.8 1.8 %collective-permute-start.3 = (bf16[512,512]{1,0:T(8,128)(2,1)}, bf16[512,512]{1,0:T(8,128)(2,1)S(1)}, u32[]{:S(2)}, u32[]{:S(2)}) collective-permute-start(bf16[512,512]{1,0:T(8,128)(2,1)} %get-tuple-element.37.grad), channel_id=1, source_target_pairs={{0,1},{1,0},{2,3},{3,2},{4,5},{5,4},{6,7},{7,6},{8,9},{9,8},{10,11... | collective-permute-start | bytes 1572872 | tf_op jit(solution)/shard_map/ppermute | solution.py:23
  26.8 1.8 %collective-permute-start.4 = (f32[1,512]{1,0:T(1,128)S(1)}, f32[1,512]{1,0:T(1,128)S(1)}, u32[]{:S(2)}, u32[]{:S(2)}) collective-permute-start(f32[1,512]{1,0:T(1,128)S(1)} %bitcast.12), channel_id=1, source_target_pairs={{0,1},{1,0},{2,3},{3,2},{4,5},{5,4},{6,7},{7,6},{8,9},{9,8},{10,11... | collective-permute-start | bytes 6152 | tf_op jit(solution)/shard_map/ppermute | solution.py:23
  29.3 6.7 %shard_map.121.term = f32[512,512]{1,0:T(8,128)} custom-call(bf16[512,512]{1,0:T(8,128)(2,1)} %copy-done.5, bf16[512,512]{1,0:T(8,128)(2,1)} %get-tuple-element.39.table.users_p, bf16[512,1024]{1,0:T(8,128)(2,1)} %get-tuple-element.34.errors_o, bf16[512,1024]{1,0:T(8,128)(2,1)} %get-tuple-element.43.errors_p, bf16[1024,512]{1,0:T(8,128)(2,1)} %get-tuple-element.32.items_b.items), custom_call_target="tpu_custom_call" | custom-call | flops 1610612736 | bytes 4194304 | tf_op jit(solution)/shard_map/pallas_call | solution.py:311
  36.0 14.3 %collective-permute-done.4.sums = f32[1,512]{1,0:T(1,128)S(1)} collective-permute-done((f32[1,512]{1,0:T(1,128)S(1)}, f32[1,512]{1,0:T(1,128)S(1)}, u32[]{:S(2)}, u32[]{:S(2)}) %collective-permute-start.4) | collective-permute-done | bytes 2080 | tf_op jit(solution)/shard_map/ppermute | solution.py:23
  51.7 3.4 %shard_map.120 = (bf16[512,512]{1,0:T(8,128)(2,1)}, bf16[512,512]{1,0:T(8,128)(2,1)}) custom-call(bf16[512,512]{1,0:T(8,128)(2,1)} %get-tuple-element.39.table.users_p, bf16[512,512]{1,0:T(8,128)(2,1)} %get-tuple-element.38.grad, bf16[512,512]{1,0:T(8,128)(2,1)} %copy-done.6, f32[1,512]{1,0:T(1,128)} %copy-done.7, bf16[512,512]{1,0:T(8,128)(2,1)} %relation.9), custom_call_target="tpu_custom_call" | custom-call | flops 268435456 | bytes 4194304 | tf_op jit(solution)/shard_map/pallas_call | solution.py:275
  55.7 9.6 %shard_map.122 = (f32[512,512]{1,0:T(8,128)}, bf16[1024,1024]{1,0:T(8,128)(2,1)}, f32[256,512]{1,0:T(8,128)}, f32[256,512]{1,0:T(8,128)}, bf16[512,512]{1,0:T(8,...) custom-call(s32[2]{0:T(128)} %pad_add_fusion.place, f32[1,512]{1,0:T(1,128)} %bitcast.11, ...), custom_call_target="tpu_custom_call" | custom-call | flops 4026531840 | bytes 4194304 | tf_op jit(solution)/shard_map/pallas_call | solution.py:403
  66.0 1.7 %collective-permute-done.10 = f32[256,512]{1,0:T(8,128)S(1)} collective-permute-done((f32[256,512]{1,0:T(8,128)}, f32[256,512]{1,0:T(8,128)S(1)}, u32[]{:S(2)}, u32[]{:S(2)}) %collective-permute-start.10) | collective-permute-done | bytes 524320 | tf_op jit(solution)/shard_map/ppermute | solution.py:23
  69.0 2.8 %collective-permute-start.11 = (bf16[64,512]{1,0:T(8,128)(2,1)S(1)}, bf16[64,512]{1,0:T(8,128)(2,1)S(1)}, u32[]{:S(2)}, u32[]{:S(2)}) collective-permute-start(bf16[64,512]{1,0:T(8,128)(2,1)S(1)} %get-tuple-element.58), channel_id=1, source_target_pairs={{0,5},{1,4},{2,7},{3,6},{4,1},{5,0},{6,3},{7,2},{8,13},{9,12},{10,... | collective-permute-start | bytes 196616 | tf_op jit(solution)/shard_map/ppermute | solution.py:23
  72.5 1.8 %collective-permute-done.11 = bf16[64,512]{1,0:T(8,128)(2,1)S(1)} collective-permute-done((bf16[64,512]{1,0:T(8,128)(2,1)S(1)}, bf16[64,512]{1,0:T(8,128)(2,1)S(1)}, u32[]{:S(2)}, u32[]{:S(2)}) %collective-permute-start.11) | collective-permute-done | bytes 65568 | tf_op jit(solution)/shard_map/ppermute | solution.py:23
  74.4 1.7 %collective-permute-done.12 = bf16[64,512]{1,0:T(8,128)(2,1)S(1)} collective-permute-done((bf16[64,512]{1,0:T(8,128)(2,1)S(1)}, bf16[64,512]{1,0:T(8,128)(2,1)S(1)}, u32[]{:S(2)}, u32[]{:S(2)}) %collective-permute-start.12) | collective-permute-done | bytes 65568 | tf_op jit(solution)/shard_map/ppermute | solution.py:23
  76.6 1.6 %collective-permute-start.14 = (bf16[64,512]{1,0:T(8,128)(2,1)S(1)}, bf16[64,512]{1,0:T(8,128)(2,1)S(1)}, u32[]{:S(2)}, u32[]{:S(2)}) collective-permute-start(bf16[64,512]{1,0:T(8,128)(2,1)S(1)} %add_convert_fusion.1), channel_id=1, source_target_pairs={{0,8},{1,9},{2,10},{3,11},{4,12},{5,13},{6,14},{7,15},{8,0},{9,1},... | collective-permute-start | bytes 196616 | tf_op jit(solution)/shard_map/ppermute | solution.py:23
  78.2 2.1 %collective-permute-start.15 = (bf16[64,512]{1,0:T(8,128)(2,1)S(1)}, bf16[64,512]{1,0:T(8,128)(2,1)S(1)}, u32[]{:S(2)}, u32[]{:S(2)}) collective-permute-start(bf16[64,512]{1,0:T(8,128)(2,1)S(1)} %add_convert_fusion.1), channel_id=1, source_target_pairs={{0,16},{1,17},{2,18},{3,19},{4,20},{5,21},{6,22},{7,23},{8,24},{9,... | collective-permute-start | bytes 196616 | tf_op jit(solution)/shard_map/ppermute | solution.py:23
  82.1 2.7 %collective-permute-done.15 = bf16[64,512]{1,0:T(8,128)(2,1)S(1)} collective-permute-done((bf16[64,512]{1,0:T(8,128)(2,1)S(1)}, bf16[64,512]{1,0:T(8,128)(2,1)S(1)}, u32[]{:S(2)}, u32[]{:S(2)}) %collective-permute-start.15) | collective-permute-done | bytes 65568 | tf_op jit(solution)/shard_map/ppermute | solution.py:23
  86.4 2.3 %collective-permute-start.17 = (bf16[64,512]{1,0:T(8,128)(2,1)S(1)}, bf16[64,512]{1,0:T(8,128)(2,1)S(1)}, u32[]{:S(2)}, u32[]{:S(2)}) collective-permute-start(bf16[64,512]{1,0:T(8,128)(2,1)S(1)} %add_convert_fusion), channel_id=1, source_target_pairs={{0,5},{1,4},{2,7},{3,6},{4,1},{5,0},{6,3},{7,2},{8,13},{9,12},{10,... | collective-permute-start | bytes 196616 | tf_op jit(solution)/shard_map/ppermute | solution.py:23
  90.0 4.7 %shard_map.123 = (f32[512,512]{1,0:T(8,128)}, bf16[512,512]{1,0:T(8,128)(2,1)}) custom-call(bf16[1024,1024]{1,0:T(8,128)(2,1)} %get-tuple-element.45.errors, bf16[1024,512]{1,0:T(8,128)(2,1)} %collective-permute-done.5.items, bf16[512,512]{1,0:T(8,128)(2,1)} %relation.9), custom_call_target="tpu_custom_call" | custom-call | flops 1610612736 | bytes 4194304 | tf_op jit(solution)/shard_map/pallas_call | solution.py:467
  94.8 1.8 %collective-permute-start.6 = (bf16[512,512]{1,0:T(8,128)(2,1)}, bf16[512,512]{1,0:T(8,128)(2,1)S(1)}, u32[]{:S(2)}, u32[]{:S(2)}) collective-permute-start(bf16[512,512]{1,0:T(8,128)(2,1)} %get-tuple-element.47), channel_id=1, source_target_pairs={{0,1},{1,0},{2,3},{3,2},{4,5},{5,4},{6,7},{7,6},{8,9},{9,8},{10,11... | collective-permute-start | bytes 1572872 | tf_op jit(solution)/shard_map/ppermute | solution.py:23
  96.6 4.4 %collective-permute-done.18 = bf16[64,512]{1,0:T(8,128)(2,1)S(1)} collective-permute-done((bf16[64,512]{1,0:T(8,128)(2,1)S(1)}, bf16[64,512]{1,0:T(8,128)(2,1)S(1)}, u32[]{:S(2)}, u32[]{:S(2)}) %collective-permute-start.18) | collective-permute-done | bytes 65568 | tf_op jit(solution)/shard_map/ppermute | solution.py:23
  101.1 5.6 %collective-permute-done.9 = f32[1,1024]{1,0:T(1,128)S(1)} collective-permute-done((f32[1,1024]{1,0:T(1,128)S(1)}, f32[1,1024]{1,0:T(1,128)S(1)}, u32[]{:S(2)}, u32[]{:S(2)}) %collective-permute-start.9) | collective-permute-done | bytes 4128 | tf_op jit(solution)/shard_map/ppermute | solution.py:32
  111.3 2.7 %maximum_convert_fusion = f32[1024,512]{1,0:T(8,128)} fusion(bf16[512,512]{1,0:T(8,128)(2,1)} %collective-permute-done.8, bf16[512,512]{1,0:T(8,128)(2,1)S(1)} %collective-permute-done.7), kind=kLoop, calls=%fused_computation | loop fusion | flops 2097152 | bytes 3145728 | tf_op jit(solution)/shard_map/concatenate | solution.py:606
  113.9 2.1 %final.1 = (f32[512,512]{1,0:T(8,128)}, f32[1,512]{1,0:T(1,128)}) custom-call(s32[2]{0:T(128)S(1)} %copy-done.3, bf16[256,512]{1,0:T(8,128)(2,1)S(1)} %pad_maximum_fusion.mine, bf16[256,512]{1,0:T(8,128)(2,1)S(1)} %collective-permute-done.20.other, f32[1,512]{1,0:T(1,128)S(1)} %bitcast.8), custom_call_target="tpu_custom_call" | custom-call | tf_op jit(solution)/shard_map/final/pallas_call | solution.py:520
  (58 shorter events, 17.5 us)
Async XLA Ops:
  1.9 15.1 %collective-permute-start = (bf16[512,512]{1,0:T(8,128)(2,1)S(1)}, bf16[512,512]{1,0:T(8,128)(2,1)}, u32[]{:S(2)}, u32[]{:S(2)}) collective-permute-start(bf16[512,512]{1,0:T(8,128)(2,1)S(1)} %convert_element_type.41.users.users_o), channel_id=1, source_target_pairs={{0,1},{1,0},{2,3},{3,2},{4,5},{5,4},{6,7},{7,6},{8,9},{9,8},{10,11... | collective-permute-start | bytes 1572872 | tf_op jit(solution)/shard_map/ppermute | solution.py:23
  17.0 9.8 %copy-start.10 = (f32[512]{0:T(512)S(1)}, f32[512]{0:T(512)}, u32[]{:S(2)}) copy-start(f32[512]{0:T(512)} %param.8) | copy-start | bytes 6148
  24.7 30.4 %collective-permute-start.5 = (bf16[1024,512]{1,0:T(8,128)(2,1)}, bf16[1024,512]{1,0:T(8,128)(2,1)}, u32[]{:S(2)}, u32[]{:S(2)}) collective-permute-start(bf16[1024,512]{1,0:T(8,128)(2,1)} %get-tuple-element.42), channel_id=1, source_target_pairs={{0,2},{2,4},{4,6},{6,8},{8,10},{10,12},{12,14},{14,16},{16,18},{18... | collective-permute-start | bytes 3145736 | tf_op jit(solution)/shard_map/ppermute | solution.py:32
  24.8 25.6 %collective-permute-start.3 = (bf16[512,512]{1,0:T(8,128)(2,1)}, bf16[512,512]{1,0:T(8,128)(2,1)S(1)}, u32[]{:S(2)}, u32[]{:S(2)}) collective-permute-start(bf16[512,512]{1,0:T(8,128)(2,1)} %get-tuple-element.37.grad), channel_id=1, source_target_pairs={{0,1},{1,0},{2,3},{3,2},{4,5},{5,4},{6,7},{7,6},{8,9},{9,8},{10,11... | collective-permute-start | bytes 1572872 | tf_op jit(solution)/shard_map/ppermute | solution.py:23
  26.6 28.5 %collective-permute-start.2 = (bf16[512,512]{1,0:T(8,128)(2,1)}, bf16[512,512]{1,0:T(8,128)(2,1)}, u32[]{:S(2)}, u32[]{:S(2)}) collective-permute-start(bf16[512,512]{1,0:T(8,128)(2,1)} %get-tuple-element.38.grad), channel_id=1, source_target_pairs={{0,1},{1,0},{2,3},{3,2},{4,5},{5,4},{6,7},{7,6},{8,9},{9,8},{10,11... | collective-permute-start | bytes 1572872 | tf_op jit(solution)/shard_map/ppermute | solution.py:23
  26.8 23.5 %collective-permute-start.4 = (f32[1,512]{1,0:T(1,128)S(1)}, f32[1,512]{1,0:T(1,128)S(1)}, u32[]{:S(2)}, u32[]{:S(2)}) collective-permute-start(f32[1,512]{1,0:T(1,128)S(1)} %bitcast.12), channel_id=1, source_target_pairs={{0,1},{1,0},{2,3},{3,2},{4,5},{5,4},{6,7},{7,6},{8,9},{9,8},{10,11... | collective-permute-start | bytes 6152 | tf_op jit(solution)/shard_map/ppermute | solution.py:23
  28.6 26.5 %collective-permute-start.1 = (f32[1,1024]{1,0:T(1,128)}, f32[1,1024]{1,0:T(1,128)S(1)}, u32[]{:S(2)}, u32[]{:S(2)}) collective-permute-start(f32[1,1024]{1,0:T(1,128)} %get-tuple-element.36), channel_id=1, source_target_pairs={{0,2},{2,4},{4,6},{6,8},{8,10},{10,12},{12,14},{14,16},{16,18},{18... | collective-permute-start | bytes 12296 | tf_op jit(solution)/shard_map/ppermute | solution.py:32
  65.3 2.5 %collective-permute-start.10 = (f32[256,512]{1,0:T(8,128)}, f32[256,512]{1,0:T(8,128)S(1)}, u32[]{:S(2)}, u32[]{:S(2)}) collective-permute-start(f32[256,512]{1,0:T(8,128)} %get-tuple-element.55), channel_id=1, source_target_pairs={{0,2},{1,3},{2,0},{3,1},{4,6},{5,7},{6,4},{7,5},{8,10},{9,11},{10,... | collective-permute-start | bytes 1572872 | tf_op jit(solution)/shard_map/ppermute | solution.py:23
  69.0 5.4 %collective-permute-start.11 = (bf16[64,512]{1,0:T(8,128)(2,1)S(1)}, bf16[64,512]{1,0:T(8,128)(2,1)S(1)}, u32[]{:S(2)}, u32[]{:S(2)}) collective-permute-start(bf16[64,512]{1,0:T(8,128)(2,1)S(1)} %get-tuple-element.58), channel_id=1, source_target_pairs={{0,5},{1,4},{2,7},{3,6},{4,1},{5,0},{6,3},{7,2},{8,13},{9,12},{10,... | collective-permute-start | bytes 196616 | tf_op jit(solution)/shard_map/ppermute | solution.py:23
  71.7 4.3 %collective-permute-start.12 = (bf16[64,512]{1,0:T(8,128)(2,1)S(1)}, bf16[64,512]{1,0:T(8,128)(2,1)S(1)}, u32[]{:S(2)}, u32[]{:S(2)}) collective-permute-start(bf16[64,512]{1,0:T(8,128)(2,1)S(1)} %get-tuple-element.60), channel_id=1, source_target_pairs={{0,1},{1,0},{2,3},{3,2},{4,5},{5,4},{6,7},{7,6},{8,9},{9,8},{10,11... | collective-permute-start | bytes 196616 | tf_op jit(solution)/shard_map/ppermute | solution.py:23
  72.3 4.3 %collective-permute-start.13 = (bf16[64,512]{1,0:T(8,128)(2,1)S(1)}, bf16[64,512]{1,0:T(8,128)(2,1)S(1)}, u32[]{:S(2)}, u32[]{:S(2)}) collective-permute-start(bf16[64,512]{1,0:T(8,128)(2,1)S(1)} %get-tuple-element.59), channel_id=1, source_target_pairs={{0,4},{1,5},{2,6},{3,7},{4,0},{5,1},{6,2},{7,3},{8,12},{9,13},{10,... | collective-permute-start | bytes 196616 | tf_op jit(solution)/shard_map/ppermute | solution.py:23
  76.6 5.5 %collective-permute-start.14 = (bf16[64,512]{1,0:T(8,128)(2,1)S(1)}, bf16[64,512]{1,0:T(8,128)(2,1)S(1)}, u32[]{:S(2)}, u32[]{:S(2)}) collective-permute-start(bf16[64,512]{1,0:T(8,128)(2,1)S(1)} %add_convert_fusion.1), channel_id=1, source_target_pairs={{0,8},{1,9},{2,10},{3,11},{4,12},{5,13},{6,14},{7,15},{8,0},{9,1},... | collective-permute-start | bytes 196616 | tf_op jit(solution)/shard_map/ppermute | solution.py:23
  78.2 6.6 %collective-permute-start.15 = (bf16[64,512]{1,0:T(8,128)(2,1)S(1)}, bf16[64,512]{1,0:T(8,128)(2,1)S(1)}, u32[]{:S(2)}, u32[]{:S(2)}) collective-permute-start(bf16[64,512]{1,0:T(8,128)(2,1)S(1)} %add_convert_fusion.1), channel_id=1, source_target_pairs={{0,16},{1,17},{2,18},{3,19},{4,20},{5,21},{6,22},{7,23},{8,24},{9,... | collective-permute-start | bytes 196616 | tf_op jit(solution)/shard_map/ppermute | solution.py:23
  80.3 6.1 %collective-permute-start.16 = (bf16[64,512]{1,0:T(8,128)(2,1)S(1)}, bf16[64,512]{1,0:T(8,128)(2,1)S(1)}, u32[]{:S(2)}, u32[]{:S(2)}) collective-permute-start(bf16[64,512]{1,0:T(8,128)(2,1)S(1)} %add_convert_fusion.1), channel_id=1, source_target_pairs={{0,24},{1,25},{2,26},{3,27},{4,28},{5,29},{6,30},{7,31},{8,16},{9,... | collective-permute-start | bytes 196616 | tf_op jit(solution)/shard_map/ppermute | solution.py:23
  81.0 30.2 %collective-permute-start.7 = (bf16[512,512]{1,0:T(8,128)(2,1)}, bf16[512,512]{1,0:T(8,128)(2,1)S(1)}, u32[]{:S(2)}, u32[]{:S(2)}) collective-permute-start(bf16[512,512]{1,0:T(8,128)(2,1)} %get-tuple-element.51), channel_id=1, source_target_pairs={{0,2},{2,4},{4,6},{6,8},{8,10},{10,12},{12,14},{14,16},{16,18},{18... | collective-permute-start | bytes 1572872 | tf_op jit(solution)/shard_map/ppermute | solution.py:32
  81.0 30.2 %collective-permute-start.8 = (bf16[512,512]{1,0:T(8,128)(2,1)}, bf16[512,512]{1,0:T(8,128)(2,1)}, u32[]{:S(2)}, u32[]{:S(2)}) collective-permute-start(bf16[512,512]{1,0:T(8,128)(2,1)} %get-tuple-element.52), channel_id=1, source_target_pairs={{0,2},{2,4},{4,6},{6,8},{8,10},{10,12},{12,14},{14,16},{16,18},{18... | collective-permute-start | bytes 1572872 | tf_op jit(solution)/shard_map/ppermute | solution.py:32
  86.4 8.3 %collective-permute-start.17 = (bf16[64,512]{1,0:T(8,128)(2,1)S(1)}, bf16[64,512]{1,0:T(8,128)(2,1)S(1)}, u32[]{:S(2)}, u32[]{:S(2)}) collective-permute-start(bf16[64,512]{1,0:T(8,128)(2,1)S(1)} %add_convert_fusion), channel_id=1, source_target_pairs={{0,5},{1,4},{2,7},{3,6},{4,1},{5,0},{6,3},{7,2},{8,13},{9,12},{10,... | collective-permute-start | bytes 196616 | tf_op jit(solution)/shard_map/ppermute | solution.py:23
  88.8 12.2 %collective-permute-start.18 = (bf16[64,512]{1,0:T(8,128)(2,1)S(1)}, bf16[64,512]{1,0:T(8,128)(2,1)S(1)}, u32[]{:S(2)}, u32[]{:S(2)}) collective-permute-start(bf16[64,512]{1,0:T(8,128)(2,1)S(1)} %add_convert_fusion), channel_id=1, source_target_pairs={{0,4},{1,5},{2,6},{3,7},{4,0},{5,1},{6,2},{7,3},{8,12},{9,13},{10,... | collective-permute-start | bytes 196616 | tf_op jit(solution)/shard_map/ppermute | solution.py:23
  89.7 11.3 %collective-permute-start.19 = (bf16[64,512]{1,0:T(8,128)(2,1)S(1)}, bf16[64,512]{1,0:T(8,128)(2,1)S(1)}, u32[]{:S(2)}, u32[]{:S(2)}) collective-permute-start(bf16[64,512]{1,0:T(8,128)(2,1)S(1)} %add_convert_fusion), channel_id=1, source_target_pairs={{0,1},{1,0},{2,3},{3,2},{4,5},{5,4},{6,7},{7,6},{8,9},{9,8},{10,11... | collective-permute-start | bytes 196616 | tf_op jit(solution)/shard_map/ppermute | solution.py:23
  90.0 11.0 %copy-start.8 = (f32[1,1024]{1,0:T(1,128)S(1)}, f32[1,1024]{1,0:T(1,128)}, u32[]{:S(2)}) copy-start(f32[1,1024]{1,0:T(1,128)} %get-tuple-element.53) | copy-start | bytes 12292
  90.0 17.3 %copy-start.4 = (f32[1,512]{1,0:T(1,128)S(1)}, f32[1,512]{1,0:T(1,128)}, u32[]{:S(2)}) copy-start(f32[1,512]{1,0:T(1,128)} %get-tuple-element.48.sums) | copy-start | bytes 6148
  94.8 12.5 %collective-permute-start.6 = (bf16[512,512]{1,0:T(8,128)(2,1)}, bf16[512,512]{1,0:T(8,128)(2,1)S(1)}, u32[]{:S(2)}, u32[]{:S(2)}) collective-permute-start(bf16[512,512]{1,0:T(8,128)(2,1)} %get-tuple-element.47), channel_id=1, source_target_pairs={{0,1},{1,0},{2,3},{3,2},{4,5},{5,4},{6,7},{7,6},{8,9},{9,8},{10,11... | collective-permute-start | bytes 1572872 | tf_op jit(solution)/shard_map/ppermute | solution.py:23
  101.0 5.7 %collective-permute-start.9 = (f32[1,1024]{1,0:T(1,128)S(1)}, f32[1,1024]{1,0:T(1,128)S(1)}, u32[]{:S(2)}, u32[]{:S(2)}) collective-permute-start(f32[1,1024]{1,0:T(1,128)S(1)} %copy-done.8), channel_id=1, source_target_pairs={{0,2},{2,4},{4,6},{6,8},{8,10},{10,12},{12,14},{14,16},{16,18},{18... | collective-permute-start | bytes 12296 | tf_op jit(solution)/shard_map/ppermute | solution.py:32
  101.0 12.9 %collective-permute-start.20 = (bf16[256,512]{1,0:T(8,128)(2,1)S(1)}, bf16[256,512]{1,0:T(8,128)(2,1)S(1)}, u32[]{:S(2)}, u32[]{:S(2)}) collective-permute-start(bf16[256,512]{1,0:T(8,128)(2,1)S(1)} %pad_maximum_fusion.mine), channel_id=1, source_target_pairs={{0,2},{1,3},{2,0},{3,1},{4,6},{5,7},{6,4},{7,5},{8,10},{9,11},{10,... | collective-permute-start | bytes 786440 | tf_op jit(solution)/shard_map/ppermute | solution.py:23
  (8 other events, 13.4 us)
